TPU v7x, 32 devices: a whole 2x2x4 slice. The times are simulated.
32 devices in a mesh: scene: 2 (over y), pulse: 4 (over z), range: 2 (over x), rep: 2 (over core).
Axes of the slice: x: 2, y: 2, z: 4, core: 2. Of those that a mesh axis runs over, the one named last changes fastest.
Arguments:
- echo: bfloat16 [8, 64, 2, 6144], P(('scene', 'pulse'), 'rep', None, 'range'), parts along dimension 0, may hold values from -6 to 6
- chirp: bfloat16 [2, 512], replicated, may hold values from -0.1875 to 0.1875
- beam_one: int32 [2, 128], replicated, may hold values from 0 to 63, as said below
- shift_one: int32 [2, 128], replicated, may hold values from -28 to 28
- frac_one: float32 [2, 128], replicated, may hold values from 0 to 1
- base_one: float32 [2, 128], replicated, may hold values from -3.140625 to 3.140625
- beam_two: int32 [2, 256], replicated, may hold values from 0 to 127, as said below
- shift_two: int32 [2, 256], replicated, may hold values from -28 to 28
- frac_two: float32 [2, 256], replicated, may hold values from 0 to 1
- base_two: float32 [2, 256], replicated, may hold values from -3.140625 to 3.140625
Outputs:
- image: bfloat16 [2, 8, 32, 2, 6144], P('rep', ('scene', 'pulse'), None, None, 'range'), parts along dimension 1
There are 2 independent parts, one for each index of `scene`. A program takes and returns all parts, laid end to end along the dimension named above; an argument that names none is the same for every part. Nothing has to cross between parts.
Inputs may be any that keep to these rules, and one draw needn't show every extreme that they name: beam_one[c, p] differs from p // 2 by at most 1 and lies in the same aligned block of 8 child beams as p // 2; the first and last parent beams read child beams 0 and 63. beam_two[c, p] differs from p // 2 by at most 1 and lies in the same aligned block of 16 child beams as p // 2; the first and last parent beams read child beams 0 and 127.
All inputs are finite; a program needn't handle non-finite values.
Results may differ from a plain program's by a relative error of at most 0.012.
Values may be sent and summed in bfloat16 or wider, within the bound.
No kernel may reach another device: no remote copies, remote signals or barrier semaphores. Data moves between devices by JAX's collectives and lax.ppermute only.
A program may use at most 64 MiB of HBM per device.

v0:
```python
import jax
import jax.numpy as jnp
from jax import lax
from jax.experimental import pallas as pl
from jax.experimental.pallas import tpu as pltpu
from jax.sharding import PartitionSpec as P

LEFT = 128
STEP = 128
ROWS = 56
COLS = 64
GROUPS = 16
RIM = 32
WIDE = GROUPS * ROWS
SPANS = COLS // GROUPS
CHUNKS = ROWS // 8
PER = 8 + 2 * CHUNKS


def exchange(parts, lane):
    parts = list(parts)
    step = 1
    while step < len(parts):
        low = (lane & step) == 0
        for first in range(len(parts)):
            if first & step:
                continue
            a, b = parts[first], parts[first + step]
            parts[first] = jnp.where(low, a, pltpu.roll(b, step, 1))
            parts[first + step] = jnp.where(low, pltpu.roll(a, 128 - step, 1), b)
        step *= 2
    return parts


def store_rimmed(ref, index, chunk, value):
    row = 8 * chunk
    ref[index, pl.ds(RIM + row, 8), :] = value
    if row >= ROWS - RIM:
        ref[index, pl.ds(row - (ROWS - RIM), 8), :] = pltpu.roll(value, 1, 1)
    if row < RIM:
        ref[index, pl.ds(RIM + ROWS + row, 8), :] = pltpu.roll(value, 127, 1)


def merged(images, index_ref, float_ref, turn_ref, entry, sign, roots):
    total = [None] * CHUNKS
    for child in range(2):
        place = entry + child
        image = index_ref[2 * place] + roots[child]
        start = index_ref[2 * place + 1]
        value = None
        for tap in range(8):
            term = images[image, pl.ds(start + tap, ROWS), :] * float_ref[PER * place + tap]
            value = term if value is None else value + term
        cos_row, sin_row = turn_ref[place, 0], turn_ref[place, 1]
        cos_signed, sin_signed = cos_row * sign, sin_row * sign
        for chunk in range(CHUNKS):
            c = float_ref[PER * place + 8 + chunk]
            s = float_ref[PER * place + 8 + CHUNKS + chunk]
            part = value[8 * chunk : 8 * chunk + 8]
            cosine = cos_row * c - sin_row * s
            sine = sin_signed * c + cos_signed * s
            term = part * cosine + pltpu.roll(part, COLS, 1) * sine
            total[chunk] = term if total[chunk] is None else total[chunk] + term
    return total


def whole_kernel(
    index_ref, float_ref, chirp_ref, a0, a1, a2, a3, turn_ref, out_ref,
    band_ref, source, columns, compressed, level_one, level_two,
):
    bins = out_ref.shape[2]
    span = band_ref.shape[1]
    lanes = lax.broadcasted_iota(jnp.int32, (8, 128), 1)
    rows = lax.broadcasted_iota(jnp.int32, (8, 128), 0)
    column = lanes & (COLS - 1)
    sign = jnp.where(lanes < COLS, -1.0, 1.0)
    first_bin, bin_total = index_ref[512], index_ref[513]
    place = column * ROWS + rows + (first_bin - LEFT)

    def inside(chunk, value):
        spot = place + 8 * chunk
        return jnp.where((spot >= 0) & (spot < bin_total), value, 0.0)

    for part in range(2):
        band = jnp.broadcast_to(chirp_ref[part : part + 1, :], (STEP, span))
        band = pltpu.roll(band, 0, 1, stride=1, stride_axis=0)
        band_ref[pl.ds(STEP * part, STEP), :] = band.astype(jnp.bfloat16)
    held = a0.shape[2]
    for pair, (near, far) in enumerate(((a0, a1), (a2, a3))):
        for comp in range(2):
            both = jnp.concatenate(
                [near[comp].astype(jnp.float32), far[comp].astype(jnp.float32)], axis=0
            ).astype(jnp.bfloat16)
            source[pair * 2 + comp, :, pl.ds(0, held)] = both
    if source.shape[2] > held:
        source[:, :, pl.ds(held, source.shape[2] - held)] = jnp.zeros(
            (4, 16, source.shape[2] - held), jnp.bfloat16
        )
    blocks = WIDE // STEP
    for pair in range(2):
        windows = jnp.concatenate(
            [
                source[pair * 2 + comp, :, pl.ds(WIDE * u + STEP * block, span)]
                for block in range(blocks)
                for comp in range(2)
                for u in range(SPANS)
            ],
            axis=0,
        )
        product = lax.dot_general(
            band_ref[...], windows, (((1,), (1,)), ((), ())), preferred_element_type=jnp.float32
        )
        wide_sign = jnp.where(lax.broadcasted_iota(jnp.int32, (STEP, 128), 1) < COLS, 1.0, -1.0)
        for block in range(blocks):
            plain = product[:STEP, 128 * block : 128 * block + 128]
            crossed = product[STEP:, 128 * block : 128 * block + 128]
            columns[pl.ds(STEP * block, STEP), :] = plain + wide_sign * pltpu.roll(crossed, COLS, 1)
        for chunk in range(CHUNKS):
            parts = [columns[pl.ds(ROWS * g + 8 * chunk, 8), :] for g in range(GROUPS)]
            for image, value in enumerate(exchange(parts, lanes)):
                store_rimmed(compressed, 16 * pair + image, chunk, inside(chunk, value))

    def one(step, carry):
        for pair in range(2):
            total = merged(
                compressed, index_ref, float_ref, turn_ref, 2 * step, sign, (16 * pair, 16 * pair)
            )
            for chunk in range(CHUNKS):
                store_rimmed(level_one, 16 * pair + step, chunk, inside(chunk, total[chunk]))
        return carry

    lax.fori_loop(0, 16, one, 0)

    for half in range(2):

        def two(step, carry):
            total = merged(
                level_one, index_ref, float_ref, turn_ref, 32 + 32 * half + 2 * step, sign, (0, 0)
            )
            for chunk in range(CHUNKS):
                level_two[step, pl.ds(8 * chunk, 8), :] = total[chunk]
            return carry

        lax.fori_loop(0, 16, two, 0)
        for chunk in range(CHUNKS):
            parts = [level_two[image, pl.ds(8 * chunk, 8), :] for image in range(GROUPS)]
            for g, value in enumerate(exchange(parts, lanes)):
                columns[pl.ds(ROWS * g + 8 * chunk, 8), :] = value
        for block in range(blocks):
            turned = columns[pl.ds(STEP * block, STEP), :].T.astype(jnp.bfloat16)
            for comp in range(2):
                for u in range(SPANS):
                    left = WIDE * u + STEP * block - LEFT
                    if 0 <= left < bins:
                        row = (comp * SPANS + u) * 16
                        out_ref[comp, pl.ds(16 * half, 16), pl.ds(left, 128)] = turned[row : row + 16]


def tables(beam, shift, frac, base, width, first_parent, first_child, swap, stride, first_bin, bin_total):
    def mine(table):
        return lax.dynamic_slice_in_dim(table, first_parent, width, 1).T

    beam, shift, frac, base = mine(beam), mine(shift), mine(frac), mine(base)
    spread = (jnp.arange(8).astype(jnp.float32) - 3.0) - frac[..., None]
    taps = jnp.sinc(spread) * (0.54 + 0.46 * jnp.cos(jnp.pi * spread / 4.0))
    slope = 0.5 * (shift.astype(jnp.float32) + frac)
    chunk_angle = slope[..., None] * (8.0 * jnp.arange(CHUNKS).astype(jnp.float32) / bin_total)
    floats = jnp.concatenate([taps, jnp.cos(chunk_angle), jnp.sin(chunk_angle)], axis=2)
    image = beam - first_child + (jnp.arange(2)[None, :] ^ swap) * stride
    indices = jnp.stack([image, shift + (RIM - 3)], axis=2)
    spot = (jnp.arange(128) % COLS)[None, :] * ROWS + jnp.arange(8)[:, None] + (first_bin - LEFT)
    ramp = spot.astype(jnp.float32) / bin_total - 0.5
    angle = base[..., None, None] + slope[..., None, None] * ramp
    turns = jnp.stack([jnp.cos(angle), jnp.sin(angle)], axis=2)
    return indices.reshape(-1), floats.reshape(-1), turns.reshape(2 * width, 2, 8, 128)


def neighbours(head, tail, axis):
    count = lax.axis_size(axis)
    index = lax.axis_index(axis)
    even = index % 2 == 0
    near = [(i, i ^ 1) for i in range(count) if i ^ 1 < count]
    far = [(i + 1, i + 2) for i in range(0, count - 2, 2)]
    far = far + [(b, a) for a, b in far]
    first = lax.ppermute(jnp.where(even, tail, head), axis, near)
    second = lax.ppermute(jnp.where(even, head, tail), axis, far) if far else jnp.zeros_like(first)
    return jnp.where(even, second, first), jnp.where(even, first, second)


def body(
    echo, chirp, beam_one, shift_one, frac_one, base_one, beam_two, shift_two, frac_two, base_two
):
    signal = echo[0]
    beams, _, bins = signal.shape
    taps = chirp.shape[1]
    span = STEP + taps
    bin_total = bins * lax.axis_size("range")
    first_bin = lax.axis_index("range") * bins
    pulse = lax.axis_index("pulse")
    low, high = pulse % 2, pulse // 2 % 2
    own = 4 * lax.axis_index("rep") + 2 * low + high

    head = signal[:, :, :span]
    tail = signal[:, :, bins - span :]
    from_left, from_right = neighbours(head, tail, "range")
    wide = jnp.concatenate([from_left[:, :, span - LEFT :], signal, from_right], axis=2)
    wide = wide.reshape(4, beams // 4, 2, wide.shape[2]).transpose(0, 2, 1, 3)

    def block_of(index):
        return lax.dynamic_index_in_dim(wide, 2 * (index % 2) + index // 2 % 2, 0, keepdims=False)

    parts = [block_of(pulse)]
    for mask in (1, 2, 3):
        route = [(i, i ^ mask) for i in range(lax.axis_size("pulse"))]
        parts.append(lax.ppermute(block_of(pulse ^ mask), "pulse", route))

    one = tables(
        beam_one, shift_one, frac_one, base_one, 16, 16 * own, 8 * own, low, 8, first_bin, bin_total
    )
    two = tables(
        beam_two, shift_two, frac_two, base_two, 32, 32 * own, 16 * own, high, 16, first_bin, bin_total
    )
    edges = jnp.stack([first_bin, jnp.asarray(bin_total)]).astype(jnp.int32)
    pad = jnp.zeros((512 - one[0].size - two[0].size,), jnp.int32)
    indices = jnp.concatenate([one[0], two[0], pad, edges])
    floats = jnp.concatenate([one[1], two[1]])
    turns = jnp.concatenate([one[2], two[2]])
    chirp_row = jnp.pad(chirp.astype(jnp.float32), ((0, 0), (0, STEP)))

    full = SPANS * WIDE + span - STEP
    vmem = pl.BlockSpec(memory_space=pltpu.VMEM)
    smem = pl.BlockSpec(memory_space=pltpu.SMEM)
    image = pl.pallas_call(
        whole_kernel,
        out_shape=jax.ShapeDtypeStruct((2, 32, bins), jnp.bfloat16),
        in_specs=[smem, smem] + [vmem] * 6,
        out_specs=vmem,
        scratch_shapes=[
            pltpu.VMEM((2 * STEP, span), jnp.bfloat16),
            pltpu.VMEM((4, 16, full), jnp.bfloat16),
            pltpu.VMEM((WIDE, 128), jnp.float32),
            pltpu.VMEM((32, ROWS + 2 * RIM, 128), jnp.float32),
            pltpu.VMEM((32, ROWS + 2 * RIM, 128), jnp.float32),
            pltpu.VMEM((16, ROWS, 128), jnp.float32),
        ],
        name="backproject",
    )(indices, floats, chirp_row, *parts, turns)
    return image.transpose(1, 0, 2)[None, None]


def solution(mesh):
    in_specs = (P(("scene", "pulse"), "rep", None, "range"),) + (P(),) * 9
    out_specs = P("rep", ("scene", "pulse"), None, None, "range")
    return jax.shard_map(body, mesh=mesh, in_specs=in_specs, out_specs=out_specs, check_vma=False)
```

profile of v0, /device:TPU:0, one launch (start us, length us, event | category | flops | bytes accessed | tf_op | source)
XLA Modules:
  0.0 45.7 jit_solution(1889679957628148748)
XLA Ops:
  0.0 0.0 copy-start
  0.0 1.1 %copy.72 = bf16[1,32,2,3072]{3,1,2,0:T(8,128)(2,1)S(1)} copy(bf16[1,32,2,3072]{3,2,1,0:T(2,128)(2,1)} %param.10) | data formatting | bytes 786432 | tf_op args[0]
  1.1 3.0 %collective-permute-start = (bf16[32,2,640]{2,0,1:T(8,128)(2,1)S(1)}, bf16[32,2,640]{2,0,1:T(8,128)(2,1)S(1)}, u32[]{:S(2)}, u32[]{:S(2)}) collective-permute-start(bf16[32,2,640]{2,0,1:T(8,128)(2,1)S(1)} %slice_select_fusion), channel_id=1, source_target_pairs={{0,2},{2,0},{1,3},{3,1},{4,6},{6,4},{5,7},{7,5},{8,10},{10,8},{9,1... | collective-permute-start | bytes 245768 | tf_op jit(solution)/shard_map/ppermute | solution.py:185
  4.2 0.0 copy-start.10
  4.2 0.0 copy-start.6
  4.2 0.7 %copy-done.10 = f32[2,256]{1,0:T(2,128)S(1)} copy-done((f32[2,256]{1,0:T(2,128)S(1)}, f32[2,256]{1,0:T(2,128)}, u32[]{:S(2)}) %copy-start.10) | copy-done | bytes 2072
  4.8 0.0 copy-done.6
  4.9 0.1 fusion.69
  4.9 0.1 copy.63
  5.0 0.0 copy-start.4
  5.0 0.0 copy-start.8
  5.0 0.7 %copy-done.4 = s32[2,128]{1,0:T(2,128)S(1)} copy-done((s32[2,128]{1,0:T(2,128)S(1)}, s32[2,128]{1,0:T(2,128)}, u32[]{:S(2)}) %copy-start.4) | copy-done | bytes 1048
  5.7 0.0 copy-done.8
  5.7 0.1 fusion.70
  5.8 0.1 copy.61
  5.9 0.1 multiply_cosine_fusion
  6.0 0.1 multiply_cosine_fusion.1
  6.2 0.1 mul.327
  6.3 0.0 copy-done
  6.3 0.1 fusion.68
  6.3 0.1 copy.62
  6.4 0.1 add.420
  6.5 0.0 copy-start.7
  6.6 0.1 mul.322
  6.6 0.6 %copy-done.7 = f32[2,128]{1,0:T(2,128)S(1)} copy-done((f32[2,128]{1,0:T(2,128)S(1)}, f32[2,128]{1,0:T(2,128)}, u32[]{:S(2)}) %copy-start.7) | copy-done | bytes 1048
  7.2 0.1 fusion.67
  7.3 0.1 copy.60
  7.4 0.1 add.411
  7.5 0.1 fusion.16
  7.6 0.1 copy.54
  7.7 0.1 reshape.129
  7.9 0.1 fusion.13
  8.0 0.1 copy.53
  8.1 0.0 copy-start.11
  8.1 0.1 reshape.128
  8.2 0.6 %copy-done.11 = s32[2,256]{1,0:T(2,128)S(1)} copy-done((s32[2,256]{1,0:T(2,128)S(1)}, s32[2,256]{1,0:T(2,128)}, u32[]{:S(2)}) %copy-start.11) | copy-done | bytes 2072
  8.8 0.1 fusion.64
  8.9 0.1 copy.52
  9.0 0.1 reshape.127
  9.1 0.0 copy-start.9
  9.1 0.7 %copy-done.9 = s32[2,128]{1,0:T(2,128)S(1)} copy-done((s32[2,128]{1,0:T(2,128)S(1)}, s32[2,128]{1,0:T(2,128)}, u32[]{:S(2)}) %copy-start.9) | copy-done | bytes 1048
  9.8 0.1 fusion.61
  9.9 0.1 copy.51
  10.0 0.1 reshape.126
  10.1 1.0 %fusion.1 = (f32[64,1,8,128]{3,2,1,0:T(8,128)S(1)}, f32[64,1,8,128]{3,2,1,0:T(8,128)S(1)}) fusion(f32[8,128]{1,0:T(8,128)S(1)} %multiply_add_fusion.4, f32[64]{0:T(128)S(1)} %mul.327, f32[64]{0:T(128)S(1)} %add.420), kind=kLoop, calls=%fused_computation.6 | loop fusion | flops 131072 | bytes 528896 | tf_op jit(solution)/shard_map/cos | solution.py:174
  11.1 0.6 %fusion.3 = (f32[32,1,8,128]{3,2,1,0:T(8,128)S(1)}, f32[32,1,8,128]{3,2,1,0:T(8,128)S(1)}) fusion(f32[8,128]{1,0:T(8,128)S(1)} %multiply_add_fusion.4, f32[32]{0:T(128)S(1)} %mul.322, f32[32]{0:T(128)S(1)} %add.411), kind=kLoop, calls=%fused_computation.9 | loop fusion | flops 65536 | bytes 266496 | tf_op jit(solution)/shard_map/cos | solution.py:174
  11.7 0.7 %pad_maximum_fusion.3.float_ref = f32[2112]{0:T(1024)} fusion(f32[1408]{0:T(1024)S(1)} %reshape.129, f32[704]{0:T(1024)S(1)} %reshape.128), kind=kLoop, calls=%fused_computation.38 | loop fusion | flops 2112 | bytes 16896 | tf_op jit(solution)/shard_map/concatenate | solution.py:226
  12.4 0.7 %concatenate.27.index_ref = s32[514]{0:T(1024)} concatenate(s32[64]{0:T(128)S(1)} %reshape.126, s32[128]{0:T(128)S(1)} %reshape.127, s32[320]{0:T(512)S(1)} %broadcast_in_dim.15, s32[1]{0:T(128)} %bitcast.8, s32[1]{0:T(128)} %constant.226.clone.1), dimensions={0} | concatenate | bytes 4112 | tf_op jit(solution)/shard_map/concatenate | solution.py:225
  13.1 0.0 copy-done.5
  13.1 0.6 %pad_convert_fusion.chirp_ref = f32[2,640]{1,0:T(2,128)} fusion(bf16[2,512]{1,0:T(2,128)(2,1)S(1)} %copy-done.5), kind=kLoop, calls=%fused_computation.104 | loop fusion | flops 1280 | bytes 7168 | tf_op jit(solution)/shard_map/jit(_pad)/pad | solution.py:228
  13.7 0.0 collective-permute-done
  13.7 0.7 %dynamic-slice_bitcast_fusion = (bf16[2,8,3840]{2,1,0:T(8,128)(2,1)S(1)}, bf16[2,8,3840]{2,1,0:T(8,128)(2,1)S(1)}, bf16[2,8,3840]{2,1,0:T(8,128)(2,1)S(1)}, bf16[2,8,3840]{2,1,0:T(8,128)(2,1)}) fusion(bf16[4,8,2,3840]{3,1,0,2:T(8,128)(2,1)S(1)} %pad_maximum_fusion, s32[]{:T(128)S(6)} %select_n.186, s32[]{:T(128)S(6)} %select_n.182, s32[]{:T(128)S(6)} %select_n.178, ...), kind=kLoop, calls=%fused_computation.10 | loop fusion | bytes 983056 | tf_op jit(solution)/shard_map/jit(dynamic_index_in_dim)/squeeze | solution.py:210
  14.4 1.6 %collective-permute-start.1 = (bf16[2,8,3840]{2,1,0:T(8,128)(2,1)S(1)}, bf16[2,8,3840]{2,1,0:T(8,128)(2,1)S(1)}, u32[]{:S(2)}, u32[]{:S(2)}) collective-permute-start(bf16[2,8,3840]{2,1,0:T(8,128)(2,1)S(1)} %get-tuple-element.11), channel_id=1, source_target_pairs={{0,4},{4,0},{8,12},{12,8},{1,5},{5,1},{9,13},{13,9},{2,6},{6,2},{1... | collective-permute-start | bytes 368648 | tf_op jit(solution)/shard_map/ppermute | solution.py:215
  16.0 2.6 %collective-permute-start.2 = (bf16[2,8,3840]{2,1,0:T(8,128)(2,1)S(1)}, bf16[2,8,3840]{2,1,0:T(8,128)(2,1)S(1)}, u32[]{:S(2)}, u32[]{:S(2)}) collective-permute-start(bf16[2,8,3840]{2,1,0:T(8,128)(2,1)S(1)} %get-tuple-element.10), channel_id=1, source_target_pairs={{0,8},{4,12},{8,0},{12,4},{1,9},{5,13},{9,1},{13,5},{2,10},{6,14},... | collective-permute-start | bytes 368648 | tf_op jit(solution)/shard_map/ppermute | solution.py:215
  18.6 0.2 collective-permute-start.3
  18.8 0.9 %maximum_maximum_fusion.turn_ref = f32[96,2,8,128]{3,2,1,0:T(8,128)} fusion(f32[64,1,8,128]{3,2,1,0:T(8,128)S(1)} %get-tuple-element.18, f32[64,1,8,128]{3,2,1,0:T(8,128)S(1)} %get-tuple-element.17, f32[32,1,8,128]{3,2,1,0:T(8,128)S(1)} %get-tuple-element.16, f32[32,1,8,128]{3,2,1,0:T(8,128)S(1)} %get-tuple-element.15), kind=kLoop, calls=%fused_computation | loop fusion | flops 589824 | bytes 1572864 | tf_op jit(solution)/shard_map/concatenate | solution.py:227
  19.8 0.9 %collective-permute-done.1.a1 = bf16[2,8,3840]{2,1,0:T(8,128)(2,1)S(1)} collective-permute-done((bf16[2,8,3840]{2,1,0:T(8,128)(2,1)S(1)}, bf16[2,8,3840]{2,1,0:T(8,128)(2,1)S(1)}, u32[]{:S(2)}, u32[]{:S(2)}) %collective-permute-start.1) | collective-permute-done | bytes 122912 | tf_op jit(solution)/shard_map/ppermute | solution.py:215
  20.7 7.4 %collective-permute-done.2.a2 = bf16[2,8,3840]{2,1,0:T(8,128)(2,1)S(1)} collective-permute-done((bf16[2,8,3840]{2,1,0:T(8,128)(2,1)S(1)}, bf16[2,8,3840]{2,1,0:T(8,128)(2,1)S(1)}, u32[]{:S(2)}, u32[]{:S(2)}) %collective-permute-start.2) | collective-permute-done | bytes 122912 | tf_op jit(solution)/shard_map/ppermute | solution.py:215
  28.1 0.0 collective-permute-done.3.a3
  28.1 0.0 copy-done.1
  28.1 0.6 %copy-done.2 = bf16[2,8,3840]{2,1,0:T(8,128)(2,1)} copy-done((bf16[2,8,3840]{2,1,0:T(8,128)(2,1)}, bf16[2,8,3840]{2,1,0:T(8,128)(2,1)S(1)}, u32[]{:S(2)}) %copy-start.2) | copy-done | bytes 122904
  28.7 0.0 copy-done.3
  28.7 14.8 %backproject.1 = bf16[2,32,3072]{2,1,0:T(8,128)(2,1)} custom-call(s32[514]{0:T(1024)} %concatenate.27.index_ref, f32[2112]{0:T(1024)} %pad_maximum_fusion.3.float_ref, f32[2,640]{1,0:T(2,128)} %pad_convert_fusion.chirp_ref, bf16[2,8,3840]{2,1,0:T(8,128)(2,1)} %get-tuple-element.12.a0, bf16[2,8,3840]{2,1,0:T(8,128)(2,1)} %copy-done.1, ...), custom_call_target="tpu_custom_call" | custom-call | tf_op jit(solution)/shard_map/backproject/pallas_call | solution.py:233
  43.6 2.1 %copy.64 = bf16[1,1,32,2,3072]{4,3,2,1,0:T(2,128)(2,1)} copy(bf16[1,1,32,2,3072]{4,2,3,1,0:T(8,128)(2,1)} %bitcast.73) | data formatting | bytes 786432 | tf_op jit(solution)/shard_map/broadcast_in_dim | solution.py:248
  (19 shorter events, 0.2 us)
Async XLA Ops:
  0.0 6.3 %copy-start = (f32[2,256]{1,0:T(2,128)S(1)}, f32[2,256]{1,0:T(2,128)}, u32[]{:S(2)}) copy-start(f32[2,256]{1,0:T(2,128)} %param.19) | copy-start | bytes 6148
  1.1 12.6 %collective-permute-start = (bf16[32,2,640]{2,0,1:T(8,128)(2,1)S(1)}, bf16[32,2,640]{2,0,1:T(8,128)(2,1)S(1)}, u32[]{:S(2)}, u32[]{:S(2)}) collective-permute-start(bf16[32,2,640]{2,0,1:T(8,128)(2,1)S(1)} %slice_select_fusion), channel_id=1, source_target_pairs={{0,2},{2,0},{1,3},{3,1},{4,6},{6,4},{5,7},{7,5},{8,10},{10,8},{9,1... | collective-permute-start | bytes 245768 | tf_op jit(solution)/shard_map/ppermute | solution.py:185
  4.2 0.7 %copy-start.10 = (f32[2,256]{1,0:T(2,128)S(1)}, f32[2,256]{1,0:T(2,128)}, u32[]{:S(2)}) copy-start(f32[2,256]{1,0:T(2,128)} %param.18) | copy-start | bytes 6148
  4.2 0.7 %copy-start.6 = (s32[2,256]{1,0:T(2,128)S(1)}, s32[2,256]{1,0:T(2,128)}, u32[]{:S(2)}) copy-start(s32[2,256]{1,0:T(2,128)} %param.17) | copy-start | bytes 6148
  5.0 0.7 %copy-start.4 = (s32[2,128]{1,0:T(2,128)S(1)}, s32[2,128]{1,0:T(2,128)}, u32[]{:S(2)}) copy-start(s32[2,128]{1,0:T(2,128)} %param.13) | copy-start | bytes 3076
  5.0 0.7 %copy-start.8 = (f32[2,128]{1,0:T(2,128)S(1)}, f32[2,128]{1,0:T(2,128)}, u32[]{:S(2)}) copy-start(f32[2,128]{1,0:T(2,128)} %param.14) | copy-start | bytes 3076
  6.5 0.7 %copy-start.7 = (f32[2,128]{1,0:T(2,128)S(1)}, f32[2,128]{1,0:T(2,128)}, u32[]{:S(2)}) copy-start(f32[2,128]{1,0:T(2,128)} %param.15) | copy-start | bytes 3076
  8.1 0.7 %copy-start.11 = (s32[2,256]{1,0:T(2,128)S(1)}, s32[2,256]{1,0:T(2,128)}, u32[]{:S(2)}) copy-start(s32[2,256]{1,0:T(2,128)} %param.16) | copy-start | bytes 6148
  9.1 0.7 %copy-start.9 = (s32[2,128]{1,0:T(2,128)S(1)}, s32[2,128]{1,0:T(2,128)}, u32[]{:S(2)}) copy-start(s32[2,128]{1,0:T(2,128)} %param.12) | copy-start | bytes 3076
  12.4 0.7 %copy-start.5 = (bf16[2,512]{1,0:T(2,128)(2,1)S(1)}, bf16[2,512]{1,0:T(2,128)(2,1)}, u32[]{:S(2)}) copy-start(bf16[2,512]{1,0:T(2,128)(2,1)} %param.11) | copy-start | bytes 6148
  14.4 6.2 %collective-permute-start.1 = (bf16[2,8,3840]{2,1,0:T(8,128)(2,1)S(1)}, bf16[2,8,3840]{2,1,0:T(8,128)(2,1)S(1)}, u32[]{:S(2)}, u32[]{:S(2)}) collective-permute-start(bf16[2,8,3840]{2,1,0:T(8,128)(2,1)S(1)} %get-tuple-element.11), channel_id=1, source_target_pairs={{0,4},{4,0},{8,12},{12,8},{1,5},{5,1},{9,13},{13,9},{2,6},{6,2},{1... | collective-permute-start | bytes 368648 | tf_op jit(solution)/shard_map/ppermute | solution.py:215
  16.0 12.0 %collective-permute-start.2 = (bf16[2,8,3840]{2,1,0:T(8,128)(2,1)S(1)}, bf16[2,8,3840]{2,1,0:T(8,128)(2,1)S(1)}, u32[]{:S(2)}, u32[]{:S(2)}) collective-permute-start(bf16[2,8,3840]{2,1,0:T(8,128)(2,1)S(1)} %get-tuple-element.10), channel_id=1, source_target_pairs={{0,8},{4,12},{8,0},{12,4},{1,9},{5,13},{9,1},{13,5},{2,10},{6,14},... | collective-permute-start | bytes 368648 | tf_op jit(solution)/shard_map/ppermute | solution.py:215
  18.6 9.4 %collective-permute-start.3 = (bf16[2,8,3840]{2,1,0:T(8,128)(2,1)S(1)}, bf16[2,8,3840]{2,1,0:T(8,128)(2,1)S(1)}, u32[]{:S(2)}, u32[]{:S(2)}) collective-permute-start(bf16[2,8,3840]{2,1,0:T(8,128)(2,1)S(1)} %get-tuple-element.9), channel_id=1, source_target_pairs={{0,12},{4,8},{8,4},{12,0},{1,13},{5,9},{9,5},{13,1},{2,14},{6,10},... | collective-permute-start | bytes 368648 | tf_op jit(solution)/shard_map/ppermute | solution.py:215
  20.7 7.4 %copy-start.1 = (bf16[2,8,3840]{2,1,0:T(8,128)(2,1)}, bf16[2,8,3840]{2,1,0:T(8,128)(2,1)S(1)}, u32[]{:S(2)}) copy-start(bf16[2,8,3840]{2,1,0:T(8,128)(2,1)S(1)} %collective-permute-done.1.a1) | copy-start | bytes 368644
  28.1 0.7 %copy-start.2 = (bf16[2,8,3840]{2,1,0:T(8,128)(2,1)}, bf16[2,8,3840]{2,1,0:T(8,128)(2,1)S(1)}, u32[]{:S(2)}) copy-start(bf16[2,8,3840]{2,1,0:T(8,128)(2,1)S(1)} %collective-permute-done.2.a2) | copy-start | bytes 368644
  28.1 0.7 %copy-start.3 = (bf16[2,8,3840]{2,1,0:T(8,128)(2,1)}, bf16[2,8,3840]{2,1,0:T(8,128)(2,1)S(1)}, u32[]{:S(2)}) copy-start(bf16[2,8,3840]{2,1,0:T(8,128)(2,1)S(1)} %collective-permute-done.3.a3) | copy-start | bytes 368644
where the time goes:
time: 46.1 us; the launch traced here: 45.7 us
  Pallas kernels  14.8 us (32%)
  local copies, waits for them, and re-layouts  10.3 us (22%)
  waiting for transfers between devices  8.29 us (18%)
  starting transfers between devices  7.42 us (16%)
  other arithmetic  4.68 us (10%)
    pallas_call x1, Pallas kernels, body(): pl.pallas_call(whole_kernel, out_shape=jax.ShapeDtypeStruct((2, 32, bins)...  14.8 us
    ppermute x3, waiting for transfers between devices, body(): parts.append(lax.ppermute(block_of(pulse ^ mask), 'pulse', route))  8.29 us
    unnamed x25, local copies, waits for them, and re-layouts  4.98 us
    ppermute x3, starting transfers between devices, body(): parts.append(lax.ppermute(block_of(pulse ^ mask), 'pulse', route))  4.39 us
    ppermute x1, starting transfers between devices, neighbours(): first = lax.ppermute(jnp.where(even, tail, head), axis, near)  3.03 us
    broadcast_in_dim x1, local copies, waits for them, and re-layouts, body(): return image.transpose(1, 0, 2)[None, None]  2.15 us
    cos x2, other arithmetic, tables(): turns = jnp.stack([jnp.cos(angle), jnp.sin(angle)], axis=2)  1.56 us
    concatenate x1, other arithmetic, body(): turns = jnp.concatenate([one[2], two[2]])  0.93 us
  transfers between devices with their start and end apart: 4, of which 2 were waited for; matrix products, arithmetic and copies ran while one was open for 15% of the time, Pallas kernels for 0%

commit v1 on v0

v1 whole, which is shorter than its diff:
```python
import jax
import jax.numpy as jnp
from jax import lax
from jax.experimental import pallas as pl
from jax.experimental.pallas import tpu as pltpu
from jax.sharding import PartitionSpec as P

LEFT = 128
STEP = 128
ROWS = 56
COLS = 64
GROUPS = 16
RIM = 32
WIDE = GROUPS * ROWS
SPANS = COLS // GROUPS
CHUNKS = ROWS // 8
BLOCKS = WIDE // STEP
ONE, TWO = 16, 32
TALL = ROWS + 2 * RIM
TOGETHER = 4


def position():
    rep, pulse = lax.axis_index("rep"), lax.axis_index("pulse")
    low, high = pulse % 2, pulse // 2 % 2
    return 4 * rep + 2 * low + high, low, high


def lane_ids(shape):
    return lax.broadcasted_iota(jnp.int32, shape, len(shape) - 1)


def row_ids(shape):
    return lax.broadcasted_iota(jnp.int32, shape, len(shape) - 2)


def exchange(parts):
    parts = list(parts)
    lane = lane_ids(parts[0].shape)
    step = 1
    while step < len(parts):
        low = (lane & step) == 0
        for first in range(len(parts)):
            if first & step:
                continue
            a, b = parts[first], parts[first + step]
            parts[first] = jnp.where(low, a, pltpu.roll(b, step, 1))
            parts[first + step] = jnp.where(low, pltpu.roll(a, 128 - step, 1), b)
        step *= 2
    return parts


def store_rimmed(ref, index, chunk, value):
    row = 8 * chunk
    ref[index, pl.ds(RIM + row, 8), :] = value
    if row >= ROWS - RIM:
        ref[index, pl.ds(row - (ROWS - RIM), 8), :] = pltpu.roll(value, 1, 1)
    if row < RIM:
        ref[index, pl.ds(RIM + ROWS + row, 8), :] = pltpu.roll(value, 127, 1)


def inside_test(bins):
    first_bin = lax.axis_index("range") * bins
    bin_total = bins * lax.axis_size("range")
    shape = (8, 128)
    place = (lane_ids(shape) & (COLS - 1)) * ROWS + row_ids(shape) + (first_bin - LEFT)

    def inside(chunk, value):
        spot = place + 8 * chunk
        return jnp.where((spot >= 0) & (spot < bin_total), value, 0.0)

    return inside


def prep_kernel(bins):
    def kernel(
        chirp_ref, shift_one, frac_one, base_one, shift_two, frac_two, base_two,
        band_ref, taps_ref, turn_ref,
    ):
        own, _, _ = position()
        first_bin = lax.axis_index("range") * bins
        bin_total = bins * lax.axis_size("range")
        span = band_ref.shape[0]
        for part in range(2):
            row = chirp_ref[part : part + 1, :].astype(jnp.float32)
            row = jnp.concatenate([row, jnp.zeros((1, STEP), jnp.float32)], axis=1)
            band = pltpu.roll(jnp.broadcast_to(row, (STEP, span)), 0, 1, stride=1, stride_axis=0)
            for block in range(span // 128):
                turned = band[:, 128 * block : 128 * block + 128].T
                band_ref[pl.ds(128 * block, 128), pl.ds(STEP * part, STEP)] = turned.astype(
                    jnp.bfloat16
                )

        shape = (8, 128)
        lane = lane_ids(shape)

        def packed(first, second):
            total = jnp.zeros(shape, jnp.float32)
            at = 0
            for ref, width in ((first, ONE), (second, TWO)):
                offset = own * width
                for child in range(2):
                    row = ref[child : child + 1, 0:128].astype(jnp.float32)
                    for block in range(1, ref.shape[1] // 128):
                        other = ref[child : child + 1, 128 * block : 128 * block + 128]
                        row = jnp.where(offset // 128 == block, other.astype(jnp.float32), row)
                    row = pltpu.roll(
                        jnp.broadcast_to(row, shape), (at + 256 - offset % 128) % 128, 1
                    )
                    total = jnp.where((lane >= at) & (lane < at + width), row, total)
                    at += width
            return total

        frac = packed(frac_one, frac_two)
        base = packed(base_one, base_two)
        slope = 0.5 * (packed(shift_one, shift_two) + frac)
        row = row_ids(shape).astype(jnp.float32)
        spread = (row - 3.0) - frac
        turned = jnp.pi * spread
        still = turned == 0.0
        safe = jnp.where(still, 1.0, turned)
        weights = jnp.where(still, 1.0, jnp.sin(safe) / safe) * (
            0.54 + 0.46 * jnp.cos(jnp.pi * spread / 4.0)
        )
        count = taps_ref.shape[0]
        square = (128, 128)
        base_rows = jnp.broadcast_to(base[0:1], square).T[:count]
        slope_rows = jnp.broadcast_to(slope[0:1], square).T[:count]
        wide = lane_ids((count, 128))
        spot = (wide & (COLS - 1)) * ROWS + (first_bin - LEFT)
        angle = base_rows + slope_rows * (spot.astype(jnp.float32) / bin_total - 0.5)
        cos_col, sin_col = jnp.cos(angle), jnp.sin(angle)
        sign = jnp.where(lane < COLS, -1.0, 1.0)
        fine = [slope * ((row + 8.0 * chunk) / bin_total) for chunk in range(CHUNKS)]
        cos_row = [jnp.cos(a) for a in fine]
        sin_row = [jnp.sin(a) for a in fine]
        for place in range(count):
            taps_ref[place] = jnp.broadcast_to(weights[:, place : place + 1], shape)
            c = jnp.broadcast_to(cos_col[place : place + 1], shape)
            s = jnp.broadcast_to(sin_col[place : place + 1], shape)
            c_signed, s_signed = c * sign, s * sign
            for chunk in range(CHUNKS):
                cb = jnp.broadcast_to(cos_row[chunk][:, place : place + 1], shape)
                sb = jnp.broadcast_to(sin_row[chunk][:, place : place + 1], shape)
                turn_ref[place, 0, pl.ds(8 * chunk, 8), :] = c * cb - s * sb
                turn_ref[place, 1, pl.ds(8 * chunk, 8), :] = s_signed * cb + c_signed * sb

    return kernel


def compress_pair(near, near_rim, far, far_rim, band_ref, source, columns, images, inside):
    held = near.shape[2]
    rim = near_rim.shape[2]

    def both(first, second, comp):
        return jnp.concatenate(
            [first[comp].astype(jnp.float32), second[comp].astype(jnp.float32)], axis=0
        ).astype(jnp.bfloat16)

    for comp in range(2):
        sides = both(near_rim, far_rim, comp)
        source[comp, :, pl.ds(0, LEFT)] = sides[:, :LEFT]
        source[comp, :, pl.ds(LEFT, held)] = both(near, far, comp)
        source[comp, :, pl.ds(LEFT + held, rim - LEFT)] = sides[:, LEFT:]
        rest = source.shape[2] - held - rim
        if rest:
            source[comp, :, pl.ds(held + rim, rest)] = jnp.zeros((16, rest), jnp.bfloat16)
    span = band_ref.shape[0]
    windows = jnp.concatenate(
        [
            source[comp, :, pl.ds(WIDE * u + STEP * block, span)]
            for block in range(BLOCKS)
            for comp in range(2)
            for u in range(SPANS)
        ],
        axis=0,
    )
    product = jnp.dot(windows, band_ref[...], preferred_element_type=jnp.float32)
    half = 16 * SPANS
    for block in range(BLOCKS):
        top = product[128 * block : 128 * block + half]
        low = product[128 * block + half : 128 * block + 128]
        result = jnp.concatenate(
            [top[:, :STEP] + low[:, STEP:], low[:, :STEP] - top[:, STEP:]], axis=0
        )
        columns[pl.ds(STEP * block, STEP), :] = result.astype(jnp.bfloat16).T.astype(jnp.float32)
    for chunk in range(0, CHUNKS, 2):
        size = min(2, CHUNKS - chunk) * 8
        parts = [columns[pl.ds(ROWS * g + 8 * chunk, size), :] for g in range(GROUPS)]
        parts = exchange([part.astype(jnp.bfloat16) for part in parts])
        for image, part in enumerate(parts):
            part = part.astype(jnp.float32)
            for extra in range(size // 8):
                value = inside(chunk + extra, part[8 * extra : 8 * extra + 8])
                store_rimmed(images, image, chunk + extra, value)


def merged(images, beam_ref, shift_ref, taps_ref, turn_ref, parent, first_parent, first_child,
           swap, stride, width, at):
    total = [None] * CHUNKS
    for child in range(2):
        place = at + child * width + parent
        image = beam_ref[child, first_parent + parent] - first_child + (child ^ swap) * stride
        start = shift_ref[child, first_parent + parent] + (RIM - 3)
        value = None
        for tap in range(8):
            term = images[image, pl.ds(start + tap, ROWS), :] * taps_ref[place, pl.ds(tap, 1), :]
            value = term if value is None else value + term
        for chunk in range(CHUNKS):
            part = value[8 * chunk : 8 * chunk + 8]
            term = (
                part * turn_ref[place, 0, pl.ds(8 * chunk, 8), :]
                + pltpu.roll(part, COLS, 1) * turn_ref[place, 1, pl.ds(8 * chunk, 8), :]
            )
            total[chunk] = term if total[chunk] is None else total[chunk] + term
    return total


def merge_one(images, beam_ref, shift_ref, taps_ref, turn_ref, result, inside):
    own, low, _ = position()

    def step(index, carry):
        for extra in range(TOGETHER):
            parent = TOGETHER * index + extra
            total = merged(
                images, beam_ref, shift_ref, taps_ref, turn_ref, parent, ONE * own, 8 * own, low, 8,
                ONE, 0,
            )
            for chunk in range(CHUNKS):
                store_rimmed(result, parent, chunk, inside(chunk, total[chunk]))
        return carry

    lax.fori_loop(0, ONE // TOGETHER, step, 0)


def first_kernel(bins):
    def kernel(
        beam_ref, shift_ref, a0, r0, a1, r1, band_ref, taps_ref, turn_ref, out_ref,
        source, columns, images,
    ):
        inside = inside_test(bins)
        compress_pair(a0, r0, a1, r1, band_ref, source, columns, images, inside)
        merge_one(images, beam_ref, shift_ref, taps_ref, turn_ref, out_ref, inside)

    return kernel


def second_kernel(bins):
    def kernel(
        beam_one, shift_one, beam_two, shift_two, a2, r2, a3, r3, band_ref, taps_ref, turn_ref,
        done_ref, out_ref, source, columns, images, level_one, level_two,
    ):
        inside = inside_test(bins)
        level_one[pl.ds(0, ONE)] = done_ref[...]
        compress_pair(a2, r2, a3, r3, band_ref, source, columns, images, inside)
        merge_one(
            images, beam_one, shift_one, taps_ref, turn_ref, level_one.at[pl.ds(ONE, ONE)], inside
        )
        own, _, high = position()
        for half in range(2):

            def step(index, carry):
                for extra in range(TOGETHER):
                    parent = TOGETHER * index + extra
                    total = merged(
                        level_one, beam_two, shift_two, taps_ref, turn_ref, parent + 16 * half,
                        TWO * own, ONE * own, high, ONE, TWO, 2 * ONE,
                    )
                    for chunk in range(CHUNKS):
                        level_two[parent, pl.ds(8 * chunk, 8), :] = total[chunk]
                return carry

            lax.fori_loop(0, 16 // TOGETHER, step, 0)
            for chunk in range(0, CHUNKS, 2):
                size = min(2, CHUNKS - chunk) * 8
                parts = [level_two[image, pl.ds(8 * chunk, size), :] for image in range(GROUPS)]
                parts = exchange([part.astype(jnp.bfloat16) for part in parts])
                for g, part in enumerate(parts):
                    columns[pl.ds(ROWS * g + 8 * chunk, size), :] = part.astype(jnp.float32)
            for block in range(BLOCKS):
                turned = columns[pl.ds(STEP * block, STEP), :].astype(jnp.bfloat16).T
                for comp in range(2):
                    for u in range(SPANS):
                        left = WIDE * u + STEP * block - LEFT
                        if 0 <= left < bins:
                            row = (comp * SPANS + u) * 16
                            out_ref[comp, pl.ds(16 * half, 16), pl.ds(left, 128)] = turned[
                                row : row + 16
                            ]

    return kernel


def neighbours(head, tail, axis):
    count = lax.axis_size(axis)
    even = lax.axis_index(axis) % 2 == 0
    near = [(i, i ^ 1) for i in range(count) if i ^ 1 < count]
    far = [(i + 1, i + 2) for i in range(0, count - 2, 2)]
    far = far + [(b, a) for a, b in far]
    first = lax.ppermute(jnp.where(even, tail, head), axis, near)
    second = lax.ppermute(jnp.where(even, head, tail), axis, far) if far else jnp.zeros_like(first)
    return jnp.where(even, second, first), jnp.where(even, first, second)


def body(
    echo, chirp, beam_one, shift_one, frac_one, base_one, beam_two, shift_two, frac_two, base_two
):
    signal = echo[0]
    beams, _, bins = signal.shape
    span = STEP + chirp.shape[1]
    pulse = lax.axis_index("pulse")

    signal = signal.reshape(4, beams // 4, 2, bins).transpose(0, 2, 1, 3)

    def routed(array):
        def block_of(index):
            return lax.dynamic_index_in_dim(array, 2 * (index % 2) + index // 2 % 2, 0, keepdims=False)

        parts = [block_of(pulse)]
        for mask in (1, 2, 3):
            route = [(i, i ^ mask) for i in range(lax.axis_size("pulse"))]
            parts.append(lax.ppermute(block_of(pulse ^ mask), "pulse", route))
        return parts

    parts = routed(signal)
    from_left, from_right = neighbours(
        signal[:, :, :, :span], signal[:, :, :, bins - span :], "range"
    )
    rims = routed(jnp.concatenate([from_left[:, :, :, span - LEFT :], from_right], axis=3))

    vmem = pl.BlockSpec(memory_space=pltpu.VMEM)
    smem = pl.BlockSpec(memory_space=pltpu.SMEM)
    params = pltpu.CompilerParams(vmem_limit_bytes=24 << 20)
    count = 2 * (ONE + TWO)
    band, taps, turns = pl.pallas_call(
        prep_kernel(bins),
        out_shape=(
            jax.ShapeDtypeStruct((span, 2 * STEP), jnp.bfloat16),
            jax.ShapeDtypeStruct((count, 8, 128), jnp.float32),
            jax.ShapeDtypeStruct((count, 2, ROWS, 128), jnp.float32),
        ),
        in_specs=[vmem] * 7,
        out_specs=(vmem,) * 3,
        compiler_params=params,
        name="prepare",
    )(chirp, shift_one, frac_one, base_one, shift_two, frac_two, base_two)

    scratch = [
        pltpu.VMEM((2, 16, SPANS * WIDE + span - STEP), jnp.bfloat16),
        pltpu.VMEM((WIDE, 128), jnp.float32),
        pltpu.VMEM((16, TALL, 128), jnp.float32),
    ]
    done = pl.pallas_call(
        first_kernel(bins),
        out_shape=jax.ShapeDtypeStruct((ONE, TALL, 128), jnp.float32),
        in_specs=[smem] * 2 + [vmem] * 7,
        out_specs=vmem,
        scratch_shapes=scratch,
        compiler_params=params,
        name="first_pair",
    )(beam_one, shift_one, parts[0], rims[0], parts[1], rims[1], band, taps, turns)
    image = pl.pallas_call(
        second_kernel(bins),
        out_shape=jax.ShapeDtypeStruct((2, 2 * 16, bins), jnp.bfloat16),
        in_specs=[smem] * 4 + [vmem] * 8,
        out_specs=vmem,
        scratch_shapes=scratch
        + [
            pltpu.VMEM((2 * ONE, TALL, 128), jnp.float32),
            pltpu.VMEM((16, ROWS, 128), jnp.float32),
        ],
        compiler_params=params,
        name="second_pair",
    )(
        beam_one, shift_one, beam_two, shift_two, parts[2], rims[2], parts[3], rims[3], band, taps,
        turns, done,
    )
    return image.transpose(1, 0, 2)[None, None]


def solution(mesh):
    in_specs = (P(("scene", "pulse"), "rep", None, "range"),) + (P(),) * 9
    out_specs = P("rep", ("scene", "pulse"), None, None, "range")
    return jax.shard_map(body, mesh=mesh, in_specs=in_specs, out_specs=out_specs, check_vma=False)
```

time: 46.1 us -> 31.6 us (0.69)
  waiting for transfers between devices: 8.29 us -> 0.02 us
  starting transfers between devices: 7.42 us -> 12.6 us
  other arithmetic: 4.68 us -> 0.06 us
  Pallas kernels: 14.8 us -> 10.8 us
  local copies, waits for them, and re-layouts: 10.3 us -> 7.71 us
    ppermute x3 -> x6, waiting for transfers between devices: 8.29 us -> 0.02 us  [routed(): parts.append(lax.ppermute(block_of(pulse ^ mask), 'pulse', route))]
    ppermute x3 -> x6, starting transfers between devices: 4.39 us -> 9.54 us  [routed(): parts.append(lax.ppermute(block_of(pulse ^ mask), 'pulse', route))]
    pallas_call x1 -> x3, Pallas kernels: 14.8 us -> 10.8 us  [the longest x1 5.87 us: body(): pl.pallas_call(second_kernel(bins), out_shape=jax.ShapeDtypeStruct((2, 2...]
    cos x4 -> x0, other arithmetic: 1.8 us -> none  [the longest x2 1.56 us: tables(): turns = jnp.stack([jnp.cos(angle), jnp.sin(angle)], axis=2)]
    concatenate x7 -> x0, other arithmetic: 1.68 us -> none  [the longest x1 0.93 us: body(): turns = jnp.concatenate([one[2], two[2]])]
    unnamed x25 -> x21, local copies, waits for them, and re-layouts: 4.98 us -> 6.53 us
    broadcast_in_dim x1, local copies, waits for them, and re-layouts: 2.15 us -> 1.15 us  [body(): return image.transpose(1, 0, 2)[None, None]]
    concatenate x3 -> x0, local copies, waits for them, and re-layouts: 0.85 us -> none  [the longest x1 0.66 us: body(): indices = jnp.concatenate([one[0], two[0], pad, edges])]
  transfers between devices with their start and end apart: 4 -> 7, of which waited for: 2 -> 0; matrix products, arithmetic and copies ran while one was open for 15% -> 0% of each run, Pallas kernels for 0% -> 16%
where the time goes in v1:
time: 31.6 us; the launch traced here: 31.3 us
  starting transfers between devices  12.6 us (40%)
  Pallas kernels  10.8 us (34%)
  local copies, waits for them, and re-layouts  7.71 us (24%)
    ppermute x6, starting transfers between devices, routed(): parts.append(lax.ppermute(block_of(pulse ^ mask), 'pulse', route))  9.54 us
    unnamed x21, local copies, waits for them, and re-layouts  6.53 us
    pallas_call x1, Pallas kernels, body(): pl.pallas_call(second_kernel(bins), out_shape=jax.ShapeDtypeStruct((2, 2...  5.87 us
    ppermute x1, starting transfers between devices, neighbours(): first = lax.ppermute(jnp.where(even, tail, head), axis, near)  3.03 us
    pallas_call x1, Pallas kernels, body(): pl.pallas_call(first_kernel(bins), out_shape=jax.ShapeDtypeStruct((ONE, T...  2.75 us
    pallas_call x1, Pallas kernels, body(): pl.pallas_call(prep_kernel(bins), out_shape=(jax.ShapeDtypeStruct((span,...  2.18 us
    broadcast_in_dim x1, local copies, waits for them, and re-layouts, body(): return image.transpose(1, 0, 2)[None, None]  1.15 us
  transfers between devices with their start and end apart: 7, of which 0 were waited for; matrix products, arithmetic and copies ran while one was open for 0% of the time, Pallas kernels for 16%

profile of v1, /device:TPU:0, one launch (start us, length us, event | category | flops | bytes accessed | tf_op | source)
XLA Modules:
  0.0 31.3 jit_solution(12382981301371029948)
XLA Ops:
  0.0 0.0 copy-start.1
  0.0 0.0 copy-start.7
  0.0 1.1 %copy.24 = bf16[1,32,2,3072]{3,1,2,0:T(8,128)(2,1)S(1)} copy(bf16[1,32,2,3072]{3,2,1,0:T(2,128)(2,1)} %param.10) | data formatting | bytes 786432 | tf_op args[0]
  1.1 3.0 %collective-permute-start.1 = (bf16[4,2,8,640]{3,2,0,1:T(8,128)(2,1)S(1)}, bf16[4,2,8,640]{3,2,0,1:T(8,128)(2,1)S(1)}, u32[]{:S(2)}, u32[]{:S(2)}) collective-permute-start(bf16[4,2,8,640]{3,2,0,1:T(8,128)(2,1)S(1)} %slice_select_fusion), channel_id=1, source_target_pairs={{0,2},{2,0},{1,3},{3,1},{4,6},{6,4},{5,7},{7,5},{8,10},{10,8},{9,1... | collective-permute-start | bytes 245768 | tf_op jit(solution)/shard_map/ppermute | solution.py:300
  4.2 1.6 %collective-permute-start.5 = (bf16[2,8,3072]{2,1,0:T(8,128)(2,1)S(1)}, bf16[2,8,3072]{2,1,0:T(8,128)(2,1)S(1)}, u32[]{:S(2)}, u32[]{:S(2)}) collective-permute-start(bf16[2,8,3072]{2,1,0:T(8,128)(2,1)S(1)} %get-tuple-element.11), channel_id=1, source_target_pairs={{0,4},{4,0},{8,12},{12,8},{1,5},{5,1},{9,13},{13,9},{2,6},{6,2},{1... | collective-permute-start | bytes 294920 | tf_op jit(solution)/shard_map/ppermute | solution.py:322
  5.8 2.5 %collective-permute-start.3 = (bf16[2,8,3072]{2,1,0:T(8,128)(2,1)S(1)}, bf16[2,8,3072]{2,1,0:T(8,128)(2,1)S(1)}, u32[]{:S(2)}, u32[]{:S(2)}) collective-permute-start(bf16[2,8,3072]{2,1,0:T(8,128)(2,1)S(1)} %get-tuple-element.13), channel_id=1, source_target_pairs={{0,12},{4,8},{8,4},{12,0},{1,13},{5,9},{9,5},{13,1},{2,14},{6,10},... | collective-permute-start | bytes 294920 | tf_op jit(solution)/shard_map/ppermute | solution.py:322
  8.3 0.1 collective-permute-start
  8.4 0.0 collective-permute-done.1
  8.5 1.9 %collective-permute-start.6 = (bf16[2,8,768]{2,1,0:T(8,128)(2,1)S(1)}, bf16[2,8,768]{2,1,0:T(8,128)(2,1)S(1)}, u32[]{:S(2)}, u32[]{:S(2)}) collective-permute-start(bf16[2,8,768]{2,1,0:T(8,128)(2,1)S(1)} %get-tuple-element.17), channel_id=1, source_target_pairs={{0,4},{4,0},{8,12},{12,8},{1,5},{5,1},{9,13},{13,9},{2,6},{6,2},{1... | collective-permute-start | bytes 73736 | tf_op jit(solution)/shard_map/ppermute | solution.py:322
  10.3 1.7 %collective-permute-start.2 = (bf16[2,8,768]{2,1,0:T(8,128)(2,1)S(1)}, bf16[2,8,768]{2,1,0:T(8,128)(2,1)S(1)}, u32[]{:S(2)}, u32[]{:S(2)}) collective-permute-start(bf16[2,8,768]{2,1,0:T(8,128)(2,1)S(1)} %get-tuple-element.18), channel_id=1, source_target_pairs={{0,8},{4,12},{8,0},{12,4},{1,9},{5,13},{9,1},{13,5},{2,10},{6,14},... | collective-permute-start | bytes 73736 | tf_op jit(solution)/shard_map/ppermute | solution.py:322
  12.0 0.0 collective-permute-done.5.a1
  12.0 1.8 %collective-permute-start.4 = (bf16[2,8,768]{2,1,0:T(8,128)(2,1)S(1)}, bf16[2,8,768]{2,1,0:T(8,128)(2,1)S(1)}, u32[]{:S(2)}, u32[]{:S(2)}) collective-permute-start(bf16[2,8,768]{2,1,0:T(8,128)(2,1)S(1)} %get-tuple-element.19), channel_id=1, source_target_pairs={{0,12},{4,8},{8,4},{12,0},{1,13},{5,9},{9,5},{13,1},{2,14},{6,10},... | collective-permute-start | bytes 73736 | tf_op jit(solution)/shard_map/ppermute | solution.py:322
  13.8 0.0 copy-start
  13.8 0.7 %copy-done = s32[2,128]{1,0:T(2,128)S(1)} copy-done((s32[2,128]{1,0:T(2,128)S(1)}, s32[2,128]{1,0:T(2,128)}, u32[]{:S(2)}) %copy-start) | copy-done | bytes 1048
  14.5 0.0 copy-start.2
  14.5 0.7 %copy-done.2 = s32[2,256]{1,0:T(2,128)S(1)} copy-done((s32[2,256]{1,0:T(2,128)S(1)}, s32[2,256]{1,0:T(2,128)}, u32[]{:S(2)}) %copy-start.2) | copy-done | bytes 2072
  15.2 0.0 copy-start.4
  15.2 0.7 %copy-done.4 = bf16[2,512]{1,0:T(2,128)(2,1)S(1)} copy-done((bf16[2,512]{1,0:T(2,128)(2,1)S(1)}, bf16[2,512]{1,0:T(2,128)(2,1)}, u32[]{:S(2)}) %copy-start.4) | copy-done | bytes 2072
  15.8 0.0 copy-start.5
  15.8 0.7 %copy-done.5 = f32[2,256]{1,0:T(2,128)S(1)} copy-done((f32[2,256]{1,0:T(2,128)S(1)}, f32[2,256]{1,0:T(2,128)}, u32[]{:S(2)}) %copy-start.5) | copy-done | bytes 2072
  16.5 0.0 copy-start.6
  16.5 0.7 %copy-done.6 = f32[2,256]{1,0:T(2,128)S(1)} copy-done((f32[2,256]{1,0:T(2,128)S(1)}, f32[2,256]{1,0:T(2,128)}, u32[]{:S(2)}) %copy-start.6) | copy-done | bytes 2072
  17.2 0.0 copy-start.8
  17.2 0.7 %copy-done.8 = f32[2,128]{1,0:T(2,128)S(1)} copy-done((f32[2,128]{1,0:T(2,128)S(1)}, f32[2,128]{1,0:T(2,128)}, u32[]{:S(2)}) %copy-start.8) | copy-done | bytes 1048
  17.9 0.0 copy-start.9
  17.9 0.7 %copy-done.9 = f32[2,128]{1,0:T(2,128)S(1)} copy-done((f32[2,128]{1,0:T(2,128)S(1)}, f32[2,128]{1,0:T(2,128)}, u32[]{:S(2)}) %copy-start.9) | copy-done | bytes 1048
  18.6 2.2 %prepare.1 = (bf16[640,256]{1,0:T(8,128)(2,1)S(1)}, f32[96,8,128]{2,1,0:T(8,128)S(1)}, f32[96,2,56,128]{3,2,1,0:T(8,128)S(1)}) custom-call(bf16[2,512]{1,0:T(2,128)(2,1)S(1)} %copy-done.4, s32[2,128]{1,0:T(2,128)S(1)} %copy-done, f32[2,128]{1,0:T(2,128)S(1)} %copy-done.8, f32[2,128]{1,0:T(2,128)S(1)} %copy-done.9, s32[2,256]{1,0:T(2,128)S(1)} %copy-done.2, ...), custom_call_target="tpu_custom_call" | custom-call | tf_op jit(solution)/shard_map/prepare/pallas_call | solution.py:335
  20.7 0.0 collective-permute-done.6.r1
  20.8 0.0 copy-start.3
  20.8 0.7 %copy-done.3 = s32[2,128]{1,0:T(2,128)S(1)} copy-done((s32[2,128]{1,0:T(2,128)S(1)}, s32[2,128]{1,0:T(2,128)}, u32[]{:S(2)}) %copy-start.3) | copy-done | bytes 1048
  21.4 2.8 %first_pair.1.done_ref = f32[16,120,128]{2,1,0:T(8,128)S(1)} custom-call(s32[2,128]{1,0:T(2,128)S(1)} %copy-done.3, s32[2,128]{1,0:T(2,128)S(1)} %copy-done, bf16[2,8,3072]{2,1,0:T(8,128)(2,1)S(1)} %get-tuple-element.12.a0, bf16[2,8,768]{2,1,0:T(8,128)(2,1)S(1)} %get-tuple-element.20.r0, bf16[2,8,3072]{2,1,0:T(8,128)(2,1)S(1)} %collective-permute-done.5.a1, ...), custom_call_target="tpu_custom_call" | custom-call | tf_op jit(solution)/shard_map/first_pair/pallas_call | solution.py:353
  24.2 0.0 collective-permute-done.3.a3
  24.2 0.0 collective-permute-done.a2
  24.2 0.0 collective-permute-done.2.r2
  24.2 0.0 collective-permute-done.4.r3
  24.2 0.0 copy-done.1
  24.2 0.0 copy-done.7
  24.2 5.9 %second_pair.1 = bf16[2,32,3072]{2,1,0:T(8,128)(2,1)S(1)} custom-call(s32[2,128]{1,0:T(2,128)S(1)} %copy-done.3, s32[2,128]{1,0:T(2,128)S(1)} %copy-done.1, s32[2,256]{1,0:T(2,128)S(1)} %copy-done.7, s32[2,256]{1,0:T(2,128)S(1)} %copy-done.2, bf16[2,8,3072]{2,1,0:T(8,128)(2,1)S(1)} %collective-permute-done.a2, ...), custom_call_target="tpu_custom_call" | custom-call | tf_op jit(solution)/shard_map/second_pair/pallas_call | solution.py:362
  30.1 1.2 %copy.17 = bf16[1,1,32,2,3072]{4,3,2,1,0:T(2,128)(2,1)} copy(bf16[1,1,32,2,3072]{4,2,3,1,0:T(8,128)(2,1)S(1)} %bitcast.41) | data formatting | bytes 786432 | tf_op jit(solution)/shard_map/broadcast_in_dim | solution.py:378
  (5 shorter events, 0.1 us)
Async XLA Ops:
  0.0 24.2 %copy-start.1 = (s32[2,128]{1,0:T(2,128)S(1)}, s32[2,128]{1,0:T(2,128)}, u32[]{:S(2)}) copy-start(s32[2,128]{1,0:T(2,128)} %shift_one.3) | copy-start | bytes 3076
  0.0 24.2 %copy-start.7 = (s32[2,256]{1,0:T(2,128)S(1)}, s32[2,256]{1,0:T(2,128)}, u32[]{:S(2)}) copy-start(s32[2,256]{1,0:T(2,128)} %beam_two.1) | copy-start | bytes 6148
  1.1 7.3 %collective-permute-start.1 = (bf16[4,2,8,640]{3,2,0,1:T(8,128)(2,1)S(1)}, bf16[4,2,8,640]{3,2,0,1:T(8,128)(2,1)S(1)}, u32[]{:S(2)}, u32[]{:S(2)}) collective-permute-start(bf16[4,2,8,640]{3,2,0,1:T(8,128)(2,1)S(1)} %slice_select_fusion), channel_id=1, source_target_pairs={{0,2},{2,0},{1,3},{3,1},{4,6},{6,4},{5,7},{7,5},{8,10},{10,8},{9,1... | collective-permute-start | bytes 245768 | tf_op jit(solution)/shard_map/ppermute | solution.py:300
  4.2 7.9 %collective-permute-start.5 = (bf16[2,8,3072]{2,1,0:T(8,128)(2,1)S(1)}, bf16[2,8,3072]{2,1,0:T(8,128)(2,1)S(1)}, u32[]{:S(2)}, u32[]{:S(2)}) collective-permute-start(bf16[2,8,3072]{2,1,0:T(8,128)(2,1)S(1)} %get-tuple-element.11), channel_id=1, source_target_pairs={{0,4},{4,0},{8,12},{12,8},{1,5},{5,1},{9,13},{13,9},{2,6},{6,2},{1... | collective-permute-start | bytes 294920 | tf_op jit(solution)/shard_map/ppermute | solution.py:322
  5.8 18.4 %collective-permute-start.3 = (bf16[2,8,3072]{2,1,0:T(8,128)(2,1)S(1)}, bf16[2,8,3072]{2,1,0:T(8,128)(2,1)S(1)}, u32[]{:S(2)}, u32[]{:S(2)}) collective-permute-start(bf16[2,8,3072]{2,1,0:T(8,128)(2,1)S(1)} %get-tuple-element.13), channel_id=1, source_target_pairs={{0,12},{4,8},{8,4},{12,0},{1,13},{5,9},{9,5},{13,1},{2,14},{6,10},... | collective-permute-start | bytes 294920 | tf_op jit(solution)/shard_map/ppermute | solution.py:322
  8.3 15.9 %collective-permute-start = (bf16[2,8,3072]{2,1,0:T(8,128)(2,1)S(1)}, bf16[2,8,3072]{2,1,0:T(8,128)(2,1)S(1)}, u32[]{:S(2)}, u32[]{:S(2)}) collective-permute-start(bf16[2,8,3072]{2,1,0:T(8,128)(2,1)S(1)} %get-tuple-element.14), channel_id=1, source_target_pairs={{0,8},{4,12},{8,0},{12,4},{1,9},{5,13},{9,1},{13,5},{2,10},{6,14},... | collective-permute-start | bytes 294920 | tf_op jit(solution)/shard_map/ppermute | solution.py:322
  8.5 12.3 %collective-permute-start.6 = (bf16[2,8,768]{2,1,0:T(8,128)(2,1)S(1)}, bf16[2,8,768]{2,1,0:T(8,128)(2,1)S(1)}, u32[]{:S(2)}, u32[]{:S(2)}) collective-permute-start(bf16[2,8,768]{2,1,0:T(8,128)(2,1)S(1)} %get-tuple-element.17), channel_id=1, source_target_pairs={{0,4},{4,0},{8,12},{12,8},{1,5},{5,1},{9,13},{13,9},{2,6},{6,2},{1... | collective-permute-start | bytes 73736 | tf_op jit(solution)/shard_map/ppermute | solution.py:322
  10.3 13.9 %collective-permute-start.2 = (bf16[2,8,768]{2,1,0:T(8,128)(2,1)S(1)}, bf16[2,8,768]{2,1,0:T(8,128)(2,1)S(1)}, u32[]{:S(2)}, u32[]{:S(2)}) collective-permute-start(bf16[2,8,768]{2,1,0:T(8,128)(2,1)S(1)} %get-tuple-element.18), channel_id=1, source_target_pairs={{0,8},{4,12},{8,0},{12,4},{1,9},{5,13},{9,1},{13,5},{2,10},{6,14},... | collective-permute-start | bytes 73736 | tf_op jit(solution)/shard_map/ppermute | solution.py:322
  12.0 12.2 %collective-permute-start.4 = (bf16[2,8,768]{2,1,0:T(8,128)(2,1)S(1)}, bf16[2,8,768]{2,1,0:T(8,128)(2,1)S(1)}, u32[]{:S(2)}, u32[]{:S(2)}) collective-permute-start(bf16[2,8,768]{2,1,0:T(8,128)(2,1)S(1)} %get-tuple-element.19), channel_id=1, source_target_pairs={{0,12},{4,8},{8,4},{12,0},{1,13},{5,9},{9,5},{13,1},{2,14},{6,10},... | collective-permute-start | bytes 73736 | tf_op jit(solution)/shard_map/ppermute | solution.py:322
  13.8 0.7 %copy-start = (s32[2,128]{1,0:T(2,128)S(1)}, s32[2,128]{1,0:T(2,128)}, u32[]{:S(2)}) copy-start(s32[2,128]{1,0:T(2,128)} %shift_one.3) | copy-start | bytes 3076
  14.5 0.7 %copy-start.2 = (s32[2,256]{1,0:T(2,128)S(1)}, s32[2,256]{1,0:T(2,128)}, u32[]{:S(2)}) copy-start(s32[2,256]{1,0:T(2,128)} %shift_two.3) | copy-start | bytes 6148
  15.2 0.7 %copy-start.4 = (bf16[2,512]{1,0:T(2,128)(2,1)S(1)}, bf16[2,512]{1,0:T(2,128)(2,1)}, u32[]{:S(2)}) copy-start(bf16[2,512]{1,0:T(2,128)(2,1)} %chirp_ref.1) | copy-start | bytes 6148
  15.8 0.7 %copy-start.5 = (f32[2,256]{1,0:T(2,128)S(1)}, f32[2,256]{1,0:T(2,128)}, u32[]{:S(2)}) copy-start(f32[2,256]{1,0:T(2,128)} %frac_two.1) | copy-start | bytes 6148
  16.5 0.7 %copy-start.6 = (f32[2,256]{1,0:T(2,128)S(1)}, f32[2,256]{1,0:T(2,128)}, u32[]{:S(2)}) copy-start(f32[2,256]{1,0:T(2,128)} %base_two.1) | copy-start | bytes 6148
  17.2 0.7 %copy-start.8 = (f32[2,128]{1,0:T(2,128)S(1)}, f32[2,128]{1,0:T(2,128)}, u32[]{:S(2)}) copy-start(f32[2,128]{1,0:T(2,128)} %frac_one.1) | copy-start | bytes 3076
  17.9 0.7 %copy-start.9 = (f32[2,128]{1,0:T(2,128)S(1)}, f32[2,128]{1,0:T(2,128)}, u32[]{:S(2)}) copy-start(f32[2,128]{1,0:T(2,128)} %base_one.1) | copy-start | bytes 3076
  20.8 0.7 %copy-start.3 = (s32[2,128]{1,0:T(2,128)S(1)}, s32[2,128]{1,0:T(2,128)}, u32[]{:S(2)}) copy-start(s32[2,128]{1,0:T(2,128)} %beam_one.1) | copy-start | bytes 3076

commit v2 on v1

--- a/solution.py
+++ b/solution.py
@@ -72,11 +72,22 @@
     return inside
 
 
+def fetch(sources, targets, sems):
+    copies = [
+        pltpu.make_async_copy(source, target, sems.at[index])
+        for index, (source, target) in enumerate(zip(sources, targets))
+    ]
+    for copy in copies:
+        copy.start()
+    for copy in copies:
+        copy.wait()
+
+
 def prep_kernel(bins):
-    def kernel(
-        chirp_ref, shift_one, frac_one, base_one, shift_two, frac_two, base_two,
-        band_ref, taps_ref, turn_ref,
-    ):
+    def kernel(*refs):
+        far, (band_ref, taps_ref, turn_ref) = refs[:7], refs[7:10]
+        chirp_ref, shift_one, frac_one, base_one, shift_two, frac_two, base_two = refs[10:17]
+        fetch(far, refs[10:17], refs[17])
         own, _, _ = position()
         first_bin = lax.axis_index("range") * bins
         bin_total = bins * lax.axis_size("range")
@@ -235,10 +246,11 @@
 
 def first_kernel(bins):
     def kernel(
-        beam_ref, shift_ref, a0, r0, a1, r1, band_ref, taps_ref, turn_ref, out_ref,
-        source, columns, images,
+        far_beam, far_shift, a0, r0, a1, r1, band_ref, taps_ref, turn_ref, out_ref,
+        source, columns, images, beam_ref, shift_ref, sems,
     ):
         inside = inside_test(bins)
+        fetch((far_beam, far_shift), (beam_ref, shift_ref), sems)
         compress_pair(a0, r0, a1, r1, band_ref, source, columns, images, inside)
         merge_one(images, beam_ref, shift_ref, taps_ref, turn_ref, out_ref, inside)
 
@@ -247,10 +259,15 @@
 
 def second_kernel(bins):
     def kernel(
-        beam_one, shift_one, beam_two, shift_two, a2, r2, a3, r3, band_ref, taps_ref, turn_ref,
-        done_ref, out_ref, source, columns, images, level_one, level_two,
+        far_beam_one, far_shift_one, far_beam_two, far_shift_two, a2, r2, a3, r3, band_ref,
+        taps_ref, turn_ref, done_ref, out_ref, source, columns, images, level_one, level_two,
+        beam_one, shift_one, beam_two, shift_two, sems,
     ):
         inside = inside_test(bins)
+        fetch(
+            (far_beam_one, far_shift_one, far_beam_two, far_shift_two),
+            (beam_one, shift_one, beam_two, shift_two), sems,
+        )
         level_one[pl.ds(0, ONE)] = done_ref[...]
         compress_pair(a2, r2, a3, r3, band_ref, source, columns, images, inside)
         merge_one(
@@ -311,6 +328,12 @@
     pulse = lax.axis_index("pulse")
 
     signal = signal.reshape(4, beams // 4, 2, bins).transpose(0, 2, 1, 3)
+    small = (
+        chirp, beam_one, shift_one, frac_one, base_one, beam_two, shift_two, frac_two, base_two
+    )
+    chirp, beam_one, shift_one, frac_one, base_one, beam_two, shift_two, frac_two, base_two = (
+        pltpu.with_memory_space_constraint(array, pltpu.HBM) for array in small
+    )
 
     def routed(array):
         def block_of(index):
@@ -329,7 +352,13 @@
     rims = routed(jnp.concatenate([from_left[:, :, :, span - LEFT :], from_right], axis=3))
 
     vmem = pl.BlockSpec(memory_space=pltpu.VMEM)
-    smem = pl.BlockSpec(memory_space=pltpu.SMEM)
+    far = pl.BlockSpec(memory_space=pltpu.HBM)
+
+    def held(space, *arrays):
+        return [space(a.shape, a.dtype) for a in arrays] + [
+            pltpu.SemaphoreType.DMA((len(arrays),))
+        ]
+
     params = pltpu.CompilerParams(vmem_limit_bytes=24 << 20)
     count = 2 * (ONE + TWO)
     band, taps, turns = pl.pallas_call(
@@ -339,8 +368,11 @@
             jax.ShapeDtypeStruct((count, 8, 128), jnp.float32),
             jax.ShapeDtypeStruct((count, 2, ROWS, 128), jnp.float32),
         ),
-        in_specs=[vmem] * 7,
+        in_specs=[far] * 7,
         out_specs=(vmem,) * 3,
+        scratch_shapes=held(
+            pltpu.VMEM, chirp, shift_one, frac_one, base_one, shift_two, frac_two, base_two
+        ),
         compiler_params=params,
         name="prepare",
     )(chirp, shift_one, frac_one, base_one, shift_two, frac_two, base_two)
@@ -353,22 +385,23 @@
     done = pl.pallas_call(
         first_kernel(bins),
         out_shape=jax.ShapeDtypeStruct((ONE, TALL, 128), jnp.float32),
-        in_specs=[smem] * 2 + [vmem] * 7,
+        in_specs=[far] * 2 + [vmem] * 7,
         out_specs=vmem,
-        scratch_shapes=scratch,
+        scratch_shapes=scratch + held(pltpu.SMEM, beam_one, shift_one),
         compiler_params=params,
         name="first_pair",
     )(beam_one, shift_one, parts[0], rims[0], parts[1], rims[1], band, taps, turns)
     image = pl.pallas_call(
         second_kernel(bins),
         out_shape=jax.ShapeDtypeStruct((2, 2 * 16, bins), jnp.bfloat16),
-        in_specs=[smem] * 4 + [vmem] * 8,
+        in_specs=[far] * 4 + [vmem] * 8,
         out_specs=vmem,
         scratch_shapes=scratch
         + [
             pltpu.VMEM((2 * ONE, TALL, 128), jnp.float32),
             pltpu.VMEM((16, ROWS, 128), jnp.float32),
-        ],
+        ]
+        + held(pltpu.SMEM, beam_one, shift_one, beam_two, shift_two),
         compiler_params=params,
         name="second_pair",
     )(

time: 31.6 us -> 27.2 us (0.86)
  local copies, waits for them, and re-layouts: 7.71 us -> 2.24 us
  Pallas kernels: 10.8 us -> 11.9 us
    unnamed x21 -> x1, local copies, waits for them, and re-layouts: 6.53 us -> 1.06 us
    pallas_call x1, Pallas kernels: 2.18 us -> 3.03 us  [body(): pl.pallas_call(prep_kernel(bins), out_shape=(jax.ShapeDtypeStruct((span,...]
  transfers between devices with their start and end apart: 7 -> 7, of which waited for: 0 -> 0; matrix products, arithmetic and copies ran while one was open for 0% -> 0% of each run, Pallas kernels for 16% -> 22%
where the time goes in v2:
time: 27.2 us; the launch traced here: 26.9 us
  starting transfers between devices  12.6 us (46%)
  Pallas kernels  11.9 us (44%)
  local copies, waits for them, and re-layouts  2.24 us (8%)
    ppermute x6, starting transfers between devices, routed(): parts.append(lax.ppermute(block_of(pulse ^ mask), 'pulse', route))  9.54 us
    pallas_call x1, Pallas kernels, body(): pl.pallas_call(second_kernel(bins), out_shape=jax.ShapeDtypeStruct((2, 2...  6.01 us
    ppermute x1, starting transfers between devices, neighbours(): first = lax.ppermute(jnp.where(even, tail, head), axis, near)  3.03 us
    pallas_call x1, Pallas kernels, body(): pl.pallas_call(prep_kernel(bins), out_shape=(jax.ShapeDtypeStruct((span,...  3.03 us
    pallas_call x1, Pallas kernels, body(): pl.pallas_call(first_kernel(bins), out_shape=jax.ShapeDtypeStruct((ONE, T...  2.9 us
    broadcast_in_dim x1, local copies, waits for them, and re-layouts, body(): return image.transpose(1, 0, 2)[None, None]  1.15 us
    unnamed x1, local copies, waits for them, and re-layouts  1.06 us
  transfers between devices with their start and end apart: 7, of which 0 were waited for; matrix products, arithmetic and copies ran while one was open for 0% of the time, Pallas kernels for 22%

profile of v2, /device:TPU:0, one launch (start us, length us, event | category | flops | bytes accessed | tf_op | source)
XLA Modules:
  0.0 26.9 jit_solution(438928886806357549)
XLA Ops:
  0.0 1.1 %copy.24 = bf16[1,32,2,3072]{3,1,2,0:T(8,128)(2,1)S(1)} copy(bf16[1,32,2,3072]{3,2,1,0:T(2,128)(2,1)} %param.10) | data formatting | bytes 786432 | tf_op args[0]
  1.1 3.0 %collective-permute-start.1 = (bf16[4,2,8,640]{3,2,0,1:T(8,128)(2,1)S(1)}, bf16[4,2,8,640]{3,2,0,1:T(8,128)(2,1)S(1)}, u32[]{:S(2)}, u32[]{:S(2)}) collective-permute-start(bf16[4,2,8,640]{3,2,0,1:T(8,128)(2,1)S(1)} %slice_select_fusion), channel_id=1, source_target_pairs={{0,2},{2,0},{1,3},{3,1},{4,6},{6,4},{5,7},{7,5},{8,10},{10,8},{9,1... | collective-permute-start | bytes 245768 | tf_op jit(solution)/shard_map/ppermute | solution.py:317
  4.2 1.6 %collective-permute-start.5 = (bf16[2,8,3072]{2,1,0:T(8,128)(2,1)S(1)}, bf16[2,8,3072]{2,1,0:T(8,128)(2,1)S(1)}, u32[]{:S(2)}, u32[]{:S(2)}) collective-permute-start(bf16[2,8,3072]{2,1,0:T(8,128)(2,1)S(1)} %get-tuple-element.11), channel_id=1, source_target_pairs={{0,4},{4,0},{8,12},{12,8},{1,5},{5,1},{9,13},{13,9},{2,6},{6,2},{1... | collective-permute-start | bytes 294920 | tf_op jit(solution)/shard_map/ppermute | solution.py:345
  5.8 2.5 %collective-permute-start.3 = (bf16[2,8,3072]{2,1,0:T(8,128)(2,1)S(1)}, bf16[2,8,3072]{2,1,0:T(8,128)(2,1)S(1)}, u32[]{:S(2)}, u32[]{:S(2)}) collective-permute-start(bf16[2,8,3072]{2,1,0:T(8,128)(2,1)S(1)} %get-tuple-element.13), channel_id=1, source_target_pairs={{0,12},{4,8},{8,4},{12,0},{1,13},{5,9},{9,5},{13,1},{2,14},{6,10},... | collective-permute-start | bytes 294920 | tf_op jit(solution)/shard_map/ppermute | solution.py:345
  8.3 0.1 collective-permute-start
  8.4 0.0 collective-permute-done.1
  8.4 1.9 %collective-permute-start.6 = (bf16[2,8,768]{2,1,0:T(8,128)(2,1)S(1)}, bf16[2,8,768]{2,1,0:T(8,128)(2,1)S(1)}, u32[]{:S(2)}, u32[]{:S(2)}) collective-permute-start(bf16[2,8,768]{2,1,0:T(8,128)(2,1)S(1)} %get-tuple-element.17), channel_id=1, source_target_pairs={{0,4},{4,0},{8,12},{12,8},{1,5},{5,1},{9,13},{13,9},{2,6},{6,2},{1... | collective-permute-start | bytes 73736 | tf_op jit(solution)/shard_map/ppermute | solution.py:345
  10.3 1.7 %collective-permute-start.2 = (bf16[2,8,768]{2,1,0:T(8,128)(2,1)S(1)}, bf16[2,8,768]{2,1,0:T(8,128)(2,1)S(1)}, u32[]{:S(2)}, u32[]{:S(2)}) collective-permute-start(bf16[2,8,768]{2,1,0:T(8,128)(2,1)S(1)} %get-tuple-element.18), channel_id=1, source_target_pairs={{0,8},{4,12},{8,0},{12,4},{1,9},{5,13},{9,1},{13,5},{2,10},{6,14},... | collective-permute-start | bytes 73736 | tf_op jit(solution)/shard_map/ppermute | solution.py:345
  12.0 0.0 collective-permute-done.5.a1
  12.0 1.8 %collective-permute-start.4 = (bf16[2,8,768]{2,1,0:T(8,128)(2,1)S(1)}, bf16[2,8,768]{2,1,0:T(8,128)(2,1)S(1)}, u32[]{:S(2)}, u32[]{:S(2)}) collective-permute-start(bf16[2,8,768]{2,1,0:T(8,128)(2,1)S(1)} %get-tuple-element.19), channel_id=1, source_target_pairs={{0,12},{4,8},{8,4},{12,0},{1,13},{5,9},{9,5},{13,1},{2,14},{6,10},... | collective-permute-start | bytes 73736 | tf_op jit(solution)/shard_map/ppermute | solution.py:345
  13.8 3.0 %prepare.1 = (bf16[640,256]{1,0:T(8,128)(2,1)S(1)}, f32[96,8,128]{2,1,0:T(8,128)S(1)}, f32[96,2,56,128]{3,2,1,0:T(8,128)S(1)}) custom-call(bf16[2,512]{1,0:T(2,128)(2,1)} %refs_0_.1, s32[2,128]{1,0:T(2,128)} %far_shift_one.1, f32[2,128]{1,0:T(2,128)} %refs_2_.1, f32[2,128]{1,0:T(2,128)} %refs_3_.1, s32[2,256]{1,0:T(2,128)} %far_shift_two.1, ...), custom_call_target="tpu_custom_call" | custom-call | tf_op jit(solution)/shard_map/prepare/pallas_call | solution.py:364
  16.8 0.0 collective-permute-done.6.r1
  16.8 2.9 %first_pair.1.done_ref = f32[16,120,128]{2,1,0:T(8,128)S(1)} custom-call(s32[2,128]{1,0:T(2,128)} %far_beam_one.1, s32[2,128]{1,0:T(2,128)} %far_shift_one.1, bf16[2,8,3072]{2,1,0:T(8,128)(2,1)S(1)} %get-tuple-element.12.a0, bf16[2,8,768]{2,1,0:T(8,128)(2,1)S(1)} %get-tuple-element.20.r0, bf16[2,8,3072]{2,1,0:T(8,128)(2,1)S(1)} %collective-permute-done.5.a1, ...), custom_call_target="tpu_custom_call" | custom-call | tf_op jit(solution)/shard_map/first_pair/pallas_call | solution.py:385
  19.7 0.0 collective-permute-done.3.a3
  19.7 0.0 collective-permute-done.a2
  19.7 0.0 collective-permute-done.2.r2
  19.7 0.0 collective-permute-done.4.r3
  19.8 6.0 %second_pair.1 = bf16[2,32,3072]{2,1,0:T(8,128)(2,1)S(1)} custom-call(s32[2,128]{1,0:T(2,128)} %far_beam_one.1, s32[2,128]{1,0:T(2,128)} %far_shift_one.1, s32[2,256]{1,0:T(2,128)} %far_beam_two.1, s32[2,256]{1,0:T(2,128)} %far_shift_two.1, bf16[2,8,3072]{2,1,0:T(8,128)(2,1)S(1)} %collective-permute-done.a2, ...), custom_call_target="tpu_custom_call" | custom-call | tf_op jit(solution)/shard_map/second_pair/pallas_call | solution.py:394
  25.8 1.2 %copy.17 = bf16[1,1,32,2,3072]{4,3,2,1,0:T(2,128)(2,1)} copy(bf16[1,1,32,2,3072]{4,2,3,1,0:T(8,128)(2,1)S(1)} %bitcast.41) | data formatting | bytes 786432 | tf_op jit(solution)/shard_map/broadcast_in_dim | solution.py:411
  (5 shorter events, 0.1 us)
Async XLA Ops:
  1.1 7.3 %collective-permute-start.1 = (bf16[4,2,8,640]{3,2,0,1:T(8,128)(2,1)S(1)}, bf16[4,2,8,640]{3,2,0,1:T(8,128)(2,1)S(1)}, u32[]{:S(2)}, u32[]{:S(2)}) collective-permute-start(bf16[4,2,8,640]{3,2,0,1:T(8,128)(2,1)S(1)} %slice_select_fusion), channel_id=1, source_target_pairs={{0,2},{2,0},{1,3},{3,1},{4,6},{6,4},{5,7},{7,5},{8,10},{10,8},{9,1... | collective-permute-start | bytes 245768 | tf_op jit(solution)/shard_map/ppermute | solution.py:317
  4.2 7.9 %collective-permute-start.5 = (bf16[2,8,3072]{2,1,0:T(8,128)(2,1)S(1)}, bf16[2,8,3072]{2,1,0:T(8,128)(2,1)S(1)}, u32[]{:S(2)}, u32[]{:S(2)}) collective-permute-start(bf16[2,8,3072]{2,1,0:T(8,128)(2,1)S(1)} %get-tuple-element.11), channel_id=1, source_target_pairs={{0,4},{4,0},{8,12},{12,8},{1,5},{5,1},{9,13},{13,9},{2,6},{6,2},{1... | collective-permute-start | bytes 294920 | tf_op jit(solution)/shard_map/ppermute | solution.py:345
  5.8 13.9 %collective-permute-start.3 = (bf16[2,8,3072]{2,1,0:T(8,128)(2,1)S(1)}, bf16[2,8,3072]{2,1,0:T(8,128)(2,1)S(1)}, u32[]{:S(2)}, u32[]{:S(2)}) collective-permute-start(bf16[2,8,3072]{2,1,0:T(8,128)(2,1)S(1)} %get-tuple-element.13), channel_id=1, source_target_pairs={{0,12},{4,8},{8,4},{12,0},{1,13},{5,9},{9,5},{13,1},{2,14},{6,10},... | collective-permute-start | bytes 294920 | tf_op jit(solution)/shard_map/ppermute | solution.py:345
  8.3 11.5 %collective-permute-start = (bf16[2,8,3072]{2,1,0:T(8,128)(2,1)S(1)}, bf16[2,8,3072]{2,1,0:T(8,128)(2,1)S(1)}, u32[]{:S(2)}, u32[]{:S(2)}) collective-permute-start(bf16[2,8,3072]{2,1,0:T(8,128)(2,1)S(1)} %get-tuple-element.14), channel_id=1, source_target_pairs={{0,8},{4,12},{8,0},{12,4},{1,9},{5,13},{9,1},{13,5},{2,10},{6,14},... | collective-permute-start | bytes 294920 | tf_op jit(solution)/shard_map/ppermute | solution.py:345
  8.4 8.3 %collective-permute-start.6 = (bf16[2,8,768]{2,1,0:T(8,128)(2,1)S(1)}, bf16[2,8,768]{2,1,0:T(8,128)(2,1)S(1)}, u32[]{:S(2)}, u32[]{:S(2)}) collective-permute-start(bf16[2,8,768]{2,1,0:T(8,128)(2,1)S(1)} %get-tuple-element.17), channel_id=1, source_target_pairs={{0,4},{4,0},{8,12},{12,8},{1,5},{5,1},{9,13},{13,9},{2,6},{6,2},{1... | collective-permute-start | bytes 73736 | tf_op jit(solution)/shard_map/ppermute | solution.py:345
  10.3 9.4 %collective-permute-start.2 = (bf16[2,8,768]{2,1,0:T(8,128)(2,1)S(1)}, bf16[2,8,768]{2,1,0:T(8,128)(2,1)S(1)}, u32[]{:S(2)}, u32[]{:S(2)}) collective-permute-start(bf16[2,8,768]{2,1,0:T(8,128)(2,1)S(1)} %get-tuple-element.18), channel_id=1, source_target_pairs={{0,8},{4,12},{8,0},{12,4},{1,9},{5,13},{9,1},{13,5},{2,10},{6,14},... | collective-permute-start | bytes 73736 | tf_op jit(solution)/shard_map/ppermute | solution.py:345
  12.0 7.7 %collective-permute-start.4 = (bf16[2,8,768]{2,1,0:T(8,128)(2,1)S(1)}, bf16[2,8,768]{2,1,0:T(8,128)(2,1)S(1)}, u32[]{:S(2)}, u32[]{:S(2)}) collective-permute-start(bf16[2,8,768]{2,1,0:T(8,128)(2,1)S(1)} %get-tuple-element.19), channel_id=1, source_target_pairs={{0,12},{4,8},{8,4},{12,0},{1,13},{5,9},{9,5},{13,1},{2,14},{6,10},... | collective-permute-start | bytes 73736 | tf_op jit(solution)/shard_map/ppermute | solution.py:345

commit v3 on v2

--- a/solution.py
+++ b/solution.py
@@ -17,7 +17,7 @@
 BLOCKS = WIDE // STEP
 ONE, TWO = 16, 32
 TALL = ROWS + 2 * RIM
-TOGETHER = 4
+TOGETHER = 8
 
 
 def position():
@@ -142,26 +142,34 @@
         angle = base_rows + slope_rows * (spot.astype(jnp.float32) / bin_total - 0.5)
         cos_col, sin_col = jnp.cos(angle), jnp.sin(angle)
         sign = jnp.where(lane < COLS, -1.0, 1.0)
-        fine = [slope * ((row + 8.0 * chunk) / bin_total) for chunk in range(CHUNKS)]
-        cos_row = [jnp.cos(a) for a in fine]
-        sin_row = [jnp.sin(a) for a in fine]
+        fine, coarse = slope * (row / bin_total), slope * (8.0 / bin_total)
+        cos_fine, sin_fine = jnp.cos(fine), jnp.sin(fine)
+        cos_coarse, sin_coarse = jnp.cos(coarse), jnp.sin(coarse)
         for place in range(count):
-            taps_ref[place] = jnp.broadcast_to(weights[:, place : place + 1], shape)
-            c = jnp.broadcast_to(cos_col[place : place + 1], shape)
-            s = jnp.broadcast_to(sin_col[place : place + 1], shape)
-            c_signed, s_signed = c * sign, s * sign
+
+            def spread_out(table):
+                return jnp.broadcast_to(table[:, place : place + 1], shape)
+
+            taps_ref[place] = spread_out(weights)
+            cos_all = jnp.broadcast_to(cos_col[place : place + 1], shape)
+            sin_all = jnp.broadcast_to(sin_col[place : place + 1], shape) * sign
+            cos_step, sin_step = spread_out(cos_fine), spread_out(sin_fine) * sign
+            cos_next, sin_next = spread_out(cos_coarse), spread_out(sin_coarse) * sign
             for chunk in range(CHUNKS):
-                cb = jnp.broadcast_to(cos_row[chunk][:, place : place + 1], shape)
-                sb = jnp.broadcast_to(sin_row[chunk][:, place : place + 1], shape)
-                turn_ref[place, 0, pl.ds(8 * chunk, 8), :] = c * cb - s * sb
-                turn_ref[place, 1, pl.ds(8 * chunk, 8), :] = s_signed * cb + c_signed * sb
+                cos_all, sin_all = (
+                    cos_all * cos_step - sin_all * sin_step,
+                    sin_all * cos_step + cos_all * sin_step,
+                )
+                turn_ref[place, 0, pl.ds(8 * chunk, 8), :] = cos_all
+                turn_ref[place, 1, pl.ds(8 * chunk, 8), :] = sin_all
+                cos_step, sin_step = cos_next, sin_next
 
     return kernel
 
 
 def compress_pair(near, near_rim, far, far_rim, band_ref, source, columns, images, inside):
     held = near.shape[2]
-    rim = near_rim.shape[2]
+    rim = near_rim.shape[-1]
 
     def both(first, second, comp):
         return jnp.concatenate(
@@ -246,12 +254,12 @@
 
 def first_kernel(bins):
     def kernel(
-        far_beam, far_shift, a0, r0, a1, r1, band_ref, taps_ref, turn_ref, out_ref,
+        far_beam, far_shift, a0, r0, a1, rims, band_ref, taps_ref, turn_ref, out_ref,
         source, columns, images, beam_ref, shift_ref, sems,
     ):
         inside = inside_test(bins)
         fetch((far_beam, far_shift), (beam_ref, shift_ref), sems)
-        compress_pair(a0, r0, a1, r1, band_ref, source, columns, images, inside)
+        compress_pair(a0, r0, a1, rims.at[0], band_ref, source, columns, images, inside)
         merge_one(images, beam_ref, shift_ref, taps_ref, turn_ref, out_ref, inside)
 
     return kernel
@@ -259,7 +267,7 @@
 
 def second_kernel(bins):
     def kernel(
-        far_beam_one, far_shift_one, far_beam_two, far_shift_two, a2, r2, a3, r3, band_ref,
+        far_beam_one, far_shift_one, far_beam_two, far_shift_two, a2, r2, a3, rims, band_ref,
         taps_ref, turn_ref, done_ref, out_ref, source, columns, images, level_one, level_two,
         beam_one, shift_one, beam_two, shift_two, sems,
     ):
@@ -269,7 +277,7 @@
             (beam_one, shift_one, beam_two, shift_two), sems,
         )
         level_one[pl.ds(0, ONE)] = done_ref[...]
-        compress_pair(a2, r2, a3, r3, band_ref, source, columns, images, inside)
+        compress_pair(a2, r2.at[0], a3, rims.at[1], band_ref, source, columns, images, inside)
         merge_one(
             images, beam_one, shift_one, taps_ref, turn_ref, level_one.at[pl.ds(ONE, ONE)], inside
         )
@@ -335,21 +343,22 @@
         pltpu.with_memory_space_constraint(array, pltpu.HBM) for array in small
     )
 
-    def routed(array):
-        def block_of(index):
-            return lax.dynamic_index_in_dim(array, 2 * (index % 2) + index // 2 % 2, 0, keepdims=False)
-
-        parts = [block_of(pulse)]
-        for mask in (1, 2, 3):
-            route = [(i, i ^ mask) for i in range(lax.axis_size("pulse"))]
-            parts.append(lax.ppermute(block_of(pulse ^ mask), "pulse", route))
-        return parts
-
-    parts = routed(signal)
+    def block_of(array, mask):
+        index = pulse ^ mask
+        return lax.dynamic_index_in_dim(array, 2 * (index % 2) + index // 2 % 2, 0, keepdims=False)
+
+    def sent(array, mask):
+        count = lax.axis_size("pulse")
+        return lax.ppermute(array, "pulse", [(i, i ^ mask) for i in range(count)])
+
+    parts = [block_of(signal, 0)]
+    parts += [sent(block_of(signal, mask), mask) for mask in (1, 2, 3)]
     from_left, from_right = neighbours(
         signal[:, :, :, :span], signal[:, :, :, bins - span :], "range"
     )
-    rims = routed(jnp.concatenate([from_left[:, :, :, span - LEFT :], from_right], axis=3))
+    rims = jnp.concatenate([from_left[:, :, :, span - LEFT :], from_right], axis=3)
+    far_rims = sent(jnp.stack([block_of(rims, 2), block_of(rims, 3)]), 2)
+    near_rims = sent(jnp.stack([block_of(rims, 1), far_rims[1]]), 1)
 
     vmem = pl.BlockSpec(memory_space=pltpu.VMEM)
     far = pl.BlockSpec(memory_space=pltpu.HBM)
@@ -390,7 +399,7 @@
         scratch_shapes=scratch + held(pltpu.SMEM, beam_one, shift_one),
         compiler_params=params,
         name="first_pair",
-    )(beam_one, shift_one, parts[0], rims[0], parts[1], rims[1], band, taps, turns)
+    )(beam_one, shift_one, parts[0], block_of(rims, 0), parts[1], near_rims, band, taps, turns)
     image = pl.pallas_call(
         second_kernel(bins),
         out_shape=jax.ShapeDtypeStruct((2, 2 * 16, bins), jnp.bfloat16),
@@ -405,7 +414,7 @@
         compiler_params=params,
         name="second_pair",
     )(
-        beam_one, shift_one, beam_two, shift_two, parts[2], rims[2], parts[3], rims[3], band, taps,
+        beam_one, shift_one, beam_two, shift_two, parts[2], far_rims, parts[3], near_rims, band, taps,
         turns, done,
     )
     return image.transpose(1, 0, 2)[None, None]
@@ -414,4 +423,5 @@
 def solution(mesh):
     in_specs = (P(("scene", "pulse"), "rep", None, "range"),) + (P(),) * 9
     out_specs = P("rep", ("scene", "pulse"), None, None, "range")
+
     return jax.shard_map(body, mesh=mesh, in_specs=in_specs, out_specs=out_specs, check_vma=False)

time: 27.2 us -> 28.6 us (1.051)
  waiting for transfers between devices: 0.02 us -> 3.01 us
  Pallas kernels: 11.9 us -> 10.7 us
  starting transfers between devices: 12.6 us -> 12.3 us
    ppermute x1, waiting for transfers between devices: 0.01 us -> 2.44 us  [neighbours(): first = lax.ppermute(jnp.where(even, tail, head), axis, near)]
    another operation x0 -> x1, local copies, waits for them, and re-layouts: none -> 1.06 us  [body(): signal = signal.reshape(4, beams // 4, 2, bins).transpose(0, 2, 1, 3)]
    unnamed x1 -> x0, local copies, waits for them, and re-layouts: 1.06 us -> none
    pallas_call x1, Pallas kernels: 3.03 us -> 2.11 us  [body(): pl.pallas_call(prep_kernel(bins), out_shape=(jax.ShapeDtypeStruct((span,...]
    ppermute x6 -> x5, waiting for transfers between devices: 0.02 us -> 0.57 us  [sent(): return lax.ppermute(array, 'pulse', [(i, i ^ mask) for i in range(count)])]
    ppermute x6 -> x5, starting transfers between devices: 9.54 us -> 9.25 us  [sent(): return lax.ppermute(array, 'pulse', [(i, i ^ mask) for i in range(count)])]
  transfers between devices with their start and end apart: 7 -> 6, of which waited for: 0 -> 2; matrix products, arithmetic and copies ran while one was open for 0% -> 0% of each run, Pallas kernels for 22% -> 17%
where the time goes in v3:
time: 28.6 us; the launch traced here: 28.4 us
  starting transfers between devices  12.3 us (43%)
  Pallas kernels  10.7 us (37%)
  waiting for transfers between devices  3.01 us (11%)
  local copies, waits for them, and re-layouts  2.24 us (8%)
    ppermute x5, starting transfers between devices, sent(): return lax.ppermute(array, 'pulse', [(i, i ^ mask) for i in range(count)])  9.25 us
    pallas_call x1, Pallas kernels, body(): pl.pallas_call(second_kernel(bins), out_shape=jax.ShapeDtypeStruct((2, 2...  5.79 us
    ppermute x1, starting transfers between devices, neighbours(): first = lax.ppermute(jnp.where(even, tail, head), axis, near)  3.03 us
    pallas_call x1, Pallas kernels, body(): pl.pallas_call(first_kernel(bins), out_shape=jax.ShapeDtypeStruct((ONE, T...  2.81 us
    ppermute x1, waiting for transfers between devices, neighbours(): first = lax.ppermute(jnp.where(even, tail, head), axis, near)  2.44 us
    pallas_call x1, Pallas kernels, body(): pl.pallas_call(prep_kernel(bins), out_shape=(jax.ShapeDtypeStruct((span,...  2.11 us
    broadcast_in_dim x1, local copies, waits for them, and re-layouts, body(): return image.transpose(1, 0, 2)[None, None]  1.15 us
    another operation x1, local copies, waits for them, and re-layouts, body(): signal = signal.reshape(4, beams // 4, 2, bins).transpose(0, 2, 1, 3)  1.06 us
  transfers between devices with their start and end apart: 6, of which 2 were waited for; matrix products, arithmetic and copies ran while one was open for 0% of the time, Pallas kernels for 17%

profile of v3, /device:TPU:0, one launch (start us, length us, event | category | flops | bytes accessed | tf_op | source)
XLA Modules:
  0.0 28.4 jit_solution(14019399946058936105)
XLA Ops:
  0.0 1.1 %copy.23 = bf16[4,8,2,3072]{3,1,2,0:T(8,128)(2,1)S(1)} copy(bf16[4,8,2,3072]{3,2,1,0:T(2,128)(2,1)} %bitcast.27) | data formatting | bytes 786432 | tf_op jit(solution)/shard_map/reshape;squeeze | solution.py:338
  1.1 3.0 %collective-permute-start.1 = (bf16[4,2,8,640]{3,2,1,0:T(8,128)(2,1)S(1)}, bf16[4,2,8,640]{3,2,1,0:T(8,128)(2,1)S(1)}, u32[]{:S(2)}, u32[]{:S(2)}) collective-permute-start(bf16[4,2,8,640]{3,2,1,0:T(8,128)(2,1)S(1)} %slice_select_fusion), channel_id=1, source_target_pairs={{0,2},{2,0},{1,3},{3,1},{4,6},{6,4},{5,7},{7,5},{8,10},{10,8},{9,1... | collective-permute-start | bytes 245768 | tf_op jit(solution)/shard_map/ppermute | solution.py:325
  4.1 2.4 %collective-permute-done.1 = bf16[4,2,8,640]{3,2,1,0:T(8,128)(2,1)S(1)} collective-permute-done((bf16[4,2,8,640]{3,2,1,0:T(8,128)(2,1)S(1)}, bf16[4,2,8,640]{3,2,1,0:T(8,128)(2,1)S(1)}, u32[]{:S(2)}, u32[]{:S(2)}) %collective-permute-start.1) | collective-permute-done | bytes 81952 | tf_op jit(solution)/shard_map/ppermute | solution.py:325
  6.6 3.2 %collective-permute-start.2 = (bf16[2,2,8,768]{3,2,1,0:T(8,128)(2,1)S(1)}, bf16[2,2,8,768]{3,2,1,0:T(8,128)(2,1)S(1)}, u32[]{:S(2)}, u32[]{:S(2)}) collective-permute-start(bf16[2,2,8,768]{3,2,1,0:T(8,128)(2,1)S(1)} %pad_maximum_fusion), channel_id=1, source_target_pairs={{0,8},{4,12},{8,0},{12,4},{1,9},{5,13},{9,1},{13,5},{2,10},{6,14},... | collective-permute-start | bytes 147464 | tf_op jit(solution)/shard_map/ppermute | solution.py:352
  9.8 1.6 %collective-permute-start.5 = (bf16[2,8,3072]{2,1,0:T(8,128)(2,1)S(1)}, bf16[2,8,3072]{2,1,0:T(8,128)(2,1)S(1)}, u32[]{:S(2)}, u32[]{:S(2)}) collective-permute-start(bf16[2,8,3072]{2,1,0:T(8,128)(2,1)S(1)} %get-tuple-element.11), channel_id=1, source_target_pairs={{0,4},{4,0},{8,12},{12,8},{1,5},{5,1},{9,13},{13,9},{2,6},{6,2},{1... | collective-permute-start | bytes 294920 | tf_op jit(solution)/shard_map/ppermute | solution.py:352
  11.5 0.0 collective-permute-start.3
  11.5 1.9 %collective-permute-start = (bf16[2,8,3072]{2,1,0:T(8,128)(2,1)S(1)}, bf16[2,8,3072]{2,1,0:T(8,128)(2,1)S(1)}, u32[]{:S(2)}, u32[]{:S(2)}) collective-permute-start(bf16[2,8,3072]{2,1,0:T(8,128)(2,1)S(1)} %get-tuple-element.14), channel_id=1, source_target_pairs={{0,8},{4,12},{8,0},{12,4},{1,9},{5,13},{9,1},{13,5},{2,10},{6,14},... | collective-permute-start | bytes 294920 | tf_op jit(solution)/shard_map/ppermute | solution.py:352
  13.4 0.0 collective-permute-done.2.r2
  13.4 2.5 %collective-permute-start.4 = (bf16[2,2,8,768]{3,2,1,0:T(8,128)(2,1)S(1)}, bf16[2,2,8,768]{3,2,1,0:T(8,128)(2,1)S(1)}, u32[]{:S(2)}, u32[]{:S(2)}) collective-permute-start(bf16[2,2,8,768]{3,2,1,0:T(8,128)(2,1)S(1)} %pad_maximum_fusion.1), channel_id=1, source_target_pairs={{0,4},{4,0},{8,12},{12,8},{1,5},{5,1},{9,13},{13,9},{2,6},{6,2},{1... | collective-permute-start | bytes 147464 | tf_op jit(solution)/shard_map/ppermute | solution.py:352
  15.9 2.1 %prepare.1 = (bf16[640,256]{1,0:T(8,128)(2,1)S(1)}, f32[96,8,128]{2,1,0:T(8,128)S(1)}, f32[96,2,56,128]{3,2,1,0:T(8,128)S(1)}) custom-call(bf16[2,512]{1,0:T(2,128)(2,1)} %refs_0_.1, s32[2,128]{1,0:T(2,128)} %far_shift_one.1, f32[2,128]{1,0:T(2,128)} %refs_2_.1, f32[2,128]{1,0:T(2,128)} %refs_3_.1, s32[2,256]{1,0:T(2,128)} %far_shift_two.1, ...), custom_call_target="tpu_custom_call" | custom-call | tf_op jit(solution)/shard_map/prepare/pallas_call | solution.py:373
  18.1 0.0 collective-permute-done.5.a1
  18.1 0.5 %collective-permute-done.4.rims = bf16[2,2,8,768]{3,2,1,0:T(8,128)(2,1)S(1)} collective-permute-done((bf16[2,2,8,768]{3,2,1,0:T(8,128)(2,1)S(1)}, bf16[2,2,8,768]{3,2,1,0:T(8,128)(2,1)S(1)}, u32[]{:S(2)}, u32[]{:S(2)}) %collective-permute-start.4) | collective-permute-done | bytes 49184 | tf_op jit(solution)/shard_map/ppermute | solution.py:352
  18.6 2.8 %first_pair.1.done_ref = f32[16,120,128]{2,1,0:T(8,128)S(1)} custom-call(s32[2,128]{1,0:T(2,128)} %far_beam_one.1, s32[2,128]{1,0:T(2,128)} %far_shift_one.1, bf16[2,8,3072]{2,1,0:T(8,128)(2,1)S(1)} %get-tuple-element.12.a0, bf16[2,8,768]{2,1,0:T(8,128)(2,1)S(1)} %get-tuple-element.17.r0, bf16[2,8,3072]{2,1,0:T(8,128)(2,1)S(1)} %collective-permute-done.5.a1, ...), custom_call_target="tpu_custom_call" | custom-call | tf_op jit(solution)/shard_map/first_pair/pallas_call | solution.py:394
  21.4 0.0 collective-permute-done.3.a3
  21.4 0.0 collective-permute-done.a2
  21.5 5.8 %second_pair.1 = bf16[2,32,3072]{2,1,0:T(8,128)(2,1)S(1)} custom-call(s32[2,128]{1,0:T(2,128)} %far_beam_one.1, s32[2,128]{1,0:T(2,128)} %far_shift_one.1, s32[2,256]{1,0:T(2,128)} %far_beam_two.1, s32[2,256]{1,0:T(2,128)} %far_shift_two.1, bf16[2,8,3072]{2,1,0:T(8,128)(2,1)S(1)} %collective-permute-done.a2, ...), custom_call_target="tpu_custom_call" | custom-call | tf_op jit(solution)/shard_map/second_pair/pallas_call | solution.py:403
  27.3 1.2 %copy.18 = bf16[1,1,32,2,3072]{4,3,2,1,0:T(2,128)(2,1)} copy(bf16[1,1,32,2,3072]{4,2,3,1,0:T(8,128)(2,1)S(1)} %bitcast.25) | data formatting | bytes 786432 | tf_op jit(solution)/shard_map/broadcast_in_dim | solution.py:420
  (8 shorter events, 0.1 us)
Async XLA Ops:
  1.1 5.5 %collective-permute-start.1 = (bf16[4,2,8,640]{3,2,1,0:T(8,128)(2,1)S(1)}, bf16[4,2,8,640]{3,2,1,0:T(8,128)(2,1)S(1)}, u32[]{:S(2)}, u32[]{:S(2)}) collective-permute-start(bf16[4,2,8,640]{3,2,1,0:T(8,128)(2,1)S(1)} %slice_select_fusion), channel_id=1, source_target_pairs={{0,2},{2,0},{1,3},{3,1},{4,6},{6,4},{5,7},{7,5},{8,10},{10,8},{9,1... | collective-permute-start | bytes 245768 | tf_op jit(solution)/shard_map/ppermute | solution.py:325
  6.6 6.7 %collective-permute-start.2 = (bf16[2,2,8,768]{3,2,1,0:T(8,128)(2,1)S(1)}, bf16[2,2,8,768]{3,2,1,0:T(8,128)(2,1)S(1)}, u32[]{:S(2)}, u32[]{:S(2)}) collective-permute-start(bf16[2,2,8,768]{3,2,1,0:T(8,128)(2,1)S(1)} %pad_maximum_fusion), channel_id=1, source_target_pairs={{0,8},{4,12},{8,0},{12,4},{1,9},{5,13},{9,1},{13,5},{2,10},{6,14},... | collective-permute-start | bytes 147464 | tf_op jit(solution)/shard_map/ppermute | solution.py:352
  9.8 8.3 %collective-permute-start.5 = (bf16[2,8,3072]{2,1,0:T(8,128)(2,1)S(1)}, bf16[2,8,3072]{2,1,0:T(8,128)(2,1)S(1)}, u32[]{:S(2)}, u32[]{:S(2)}) collective-permute-start(bf16[2,8,3072]{2,1,0:T(8,128)(2,1)S(1)} %get-tuple-element.11), channel_id=1, source_target_pairs={{0,4},{4,0},{8,12},{12,8},{1,5},{5,1},{9,13},{13,9},{2,6},{6,2},{1... | collective-permute-start | bytes 294920 | tf_op jit(solution)/shard_map/ppermute | solution.py:352
  11.5 10.0 %collective-permute-start.3 = (bf16[2,8,3072]{2,1,0:T(8,128)(2,1)S(1)}, bf16[2,8,3072]{2,1,0:T(8,128)(2,1)S(1)}, u32[]{:S(2)}, u32[]{:S(2)}) collective-permute-start(bf16[2,8,3072]{2,1,0:T(8,128)(2,1)S(1)} %get-tuple-element.13), channel_id=1, source_target_pairs={{0,12},{4,8},{8,4},{12,0},{1,13},{5,9},{9,5},{13,1},{2,14},{6,10},... | collective-permute-start | bytes 294920 | tf_op jit(solution)/shard_map/ppermute | solution.py:352
  11.5 10.0 %collective-permute-start = (bf16[2,8,3072]{2,1,0:T(8,128)(2,1)S(1)}, bf16[2,8,3072]{2,1,0:T(8,128)(2,1)S(1)}, u32[]{:S(2)}, u32[]{:S(2)}) collective-permute-start(bf16[2,8,3072]{2,1,0:T(8,128)(2,1)S(1)} %get-tuple-element.14), channel_id=1, source_target_pairs={{0,8},{4,12},{8,0},{12,4},{1,9},{5,13},{9,1},{13,5},{2,10},{6,14},... | collective-permute-start | bytes 294920 | tf_op jit(solution)/shard_map/ppermute | solution.py:352
  13.4 5.2 %collective-permute-start.4 = (bf16[2,2,8,768]{3,2,1,0:T(8,128)(2,1)S(1)}, bf16[2,2,8,768]{3,2,1,0:T(8,128)(2,1)S(1)}, u32[]{:S(2)}, u32[]{:S(2)}) collective-permute-start(bf16[2,2,8,768]{3,2,1,0:T(8,128)(2,1)S(1)} %pad_maximum_fusion.1), channel_id=1, source_target_pairs={{0,4},{4,0},{8,12},{12,8},{1,5},{5,1},{9,13},{13,9},{2,6},{6,2},{1... | collective-permute-start | bytes 147464 | tf_op jit(solution)/shard_map/ppermute | solution.py:352

commit v4 on v3

--- a/solution.py
+++ b/solution.py
@@ -167,23 +167,26 @@
     return kernel
 
 
-def compress_pair(near, near_rim, far, far_rim, band_ref, source, columns, images, inside):
-    held = near.shape[2]
-    rim = near_rim.shape[-1]
-
-    def both(first, second, comp):
-        return jnp.concatenate(
-            [first[comp].astype(jnp.float32), second[comp].astype(jnp.float32)], axis=0
-        ).astype(jnp.bfloat16)
+def compress_pair(near, far, bins, band_ref, source, columns, images, inside):
+    rest = source.shape[2] - LEFT - bins
+    wide = near[0].shape[2] - LEFT - bins
+
+    def piece(held, comp, at, size):
+        if len(held) == 1:
+            return held[0][comp, :, pl.ds(at, size)]
+        main, rim = held
+        if at == LEFT:
+            return main[comp]
+        return rim[comp, :, pl.ds(min(at, LEFT), size)]
 
     for comp in range(2):
-        sides = both(near_rim, far_rim, comp)
-        source[comp, :, pl.ds(0, LEFT)] = sides[:, :LEFT]
-        source[comp, :, pl.ds(LEFT, held)] = both(near, far, comp)
-        source[comp, :, pl.ds(LEFT + held, rim - LEFT)] = sides[:, LEFT:]
-        rest = source.shape[2] - held - rim
-        if rest:
-            source[comp, :, pl.ds(held + rim, rest)] = jnp.zeros((16, rest), jnp.bfloat16)
+        for at, size in ((0, LEFT), (LEFT, bins), (LEFT + bins, wide)):
+            sides = [piece(held, comp, at, size).astype(jnp.float32) for held in (near, far)]
+            source[comp, :, pl.ds(at, size)] = jnp.concatenate(sides, axis=0).astype(jnp.bfloat16)
+        if rest > wide:
+            source[comp, :, pl.ds(LEFT + bins + wide, rest - wide)] = jnp.zeros(
+                (16, rest - wide), jnp.bfloat16
+            )
     span = band_ref.shape[0]
     windows = jnp.concatenate(
         [
@@ -254,12 +257,12 @@
 
 def first_kernel(bins):
     def kernel(
-        far_beam, far_shift, a0, r0, a1, rims, band_ref, taps_ref, turn_ref, out_ref,
+        far_beam, far_shift, a0, a1, band_ref, taps_ref, turn_ref, out_ref,
         source, columns, images, beam_ref, shift_ref, sems,
     ):
         inside = inside_test(bins)
         fetch((far_beam, far_shift), (beam_ref, shift_ref), sems)
-        compress_pair(a0, r0, a1, rims.at[0], band_ref, source, columns, images, inside)
+        compress_pair((a0,), (a1,), bins, band_ref, source, columns, images, inside)
         merge_one(images, beam_ref, shift_ref, taps_ref, turn_ref, out_ref, inside)
 
     return kernel
@@ -267,7 +270,7 @@
 
 def second_kernel(bins):
     def kernel(
-        far_beam_one, far_shift_one, far_beam_two, far_shift_two, a2, r2, a3, rims, band_ref,
+        far_beam_one, far_shift_one, far_beam_two, far_shift_two, a2, a3, r3, band_ref,
         taps_ref, turn_ref, done_ref, out_ref, source, columns, images, level_one, level_two,
         beam_one, shift_one, beam_two, shift_two, sems,
     ):
@@ -277,7 +280,7 @@
             (beam_one, shift_one, beam_two, shift_two), sems,
         )
         level_one[pl.ds(0, ONE)] = done_ref[...]
-        compress_pair(a2, r2.at[0], a3, rims.at[1], band_ref, source, columns, images, inside)
+        compress_pair((a2,), (a3, r3), bins, band_ref, source, columns, images, inside)
         merge_one(
             images, beam_one, shift_one, taps_ref, turn_ref, level_one.at[pl.ds(ONE, ONE)], inside
         )
@@ -351,14 +354,15 @@
         count = lax.axis_size("pulse")
         return lax.ppermute(array, "pulse", [(i, i ^ mask) for i in range(count)])
 
-    parts = [block_of(signal, 0)]
-    parts += [sent(block_of(signal, mask), mask) for mask in (1, 2, 3)]
+    far_main = sent(block_of(signal, 3), 3)
     from_left, from_right = neighbours(
         signal[:, :, :, :span], signal[:, :, :, bins - span :], "range"
     )
-    rims = jnp.concatenate([from_left[:, :, :, span - LEFT :], from_right], axis=3)
-    far_rims = sent(jnp.stack([block_of(rims, 2), block_of(rims, 3)]), 2)
-    near_rims = sent(jnp.stack([block_of(rims, 1), far_rims[1]]), 1)
+    from_left = from_left[:, :, :, span - LEFT :]
+    wide = jnp.concatenate([from_left, signal, from_right], axis=3)
+    rims = jnp.concatenate([from_left, from_right], axis=3)
+    parts = [block_of(wide, 0)] + [sent(block_of(wide, mask), mask) for mask in (1, 2)]
+    far_rim = sent(block_of(rims, 3), 3)
 
     vmem = pl.BlockSpec(memory_space=pltpu.VMEM)
     far = pl.BlockSpec(memory_space=pltpu.HBM)
@@ -394,16 +398,16 @@
     done = pl.pallas_call(
         first_kernel(bins),
         out_shape=jax.ShapeDtypeStruct((ONE, TALL, 128), jnp.float32),
-        in_specs=[far] * 2 + [vmem] * 7,
+        in_specs=[far] * 2 + [vmem] * 5,
         out_specs=vmem,
         scratch_shapes=scratch + held(pltpu.SMEM, beam_one, shift_one),
         compiler_params=params,
         name="first_pair",
-    )(beam_one, shift_one, parts[0], block_of(rims, 0), parts[1], near_rims, band, taps, turns)
+    )(beam_one, shift_one, parts[0], parts[1], band, taps, turns)
     image = pl.pallas_call(
         second_kernel(bins),
         out_shape=jax.ShapeDtypeStruct((2, 2 * 16, bins), jnp.bfloat16),
-        in_specs=[far] * 4 + [vmem] * 8,
+        in_specs=[far] * 4 + [vmem] * 7,
         out_specs=vmem,
         scratch_shapes=scratch
         + [
@@ -414,7 +418,7 @@
         compiler_params=params,
         name="second_pair",
     )(
-        beam_one, shift_one, beam_two, shift_two, parts[2], far_rims, parts[3], near_rims, band, taps,
+        beam_one, shift_one, beam_two, shift_two, parts[2], far_main, far_rim, band, taps,
         turns, done,
     )
     return image.transpose(1, 0, 2)[None, None]

time: 28.6 us -> 25.1 us (0.88)
  waiting for transfers between devices: 3.01 us -> 0.66 us
  starting transfers between devices: 12.3 us -> 11.1 us
    ppermute x1, waiting for transfers between devices: 2.44 us -> 0.01 us  [neighbours(): first = lax.ppermute(jnp.where(even, tail, head), axis, near)]
    ppermute x5 -> x4, starting transfers between devices: 9.25 us -> 8.11 us  [sent(): return lax.ppermute(array, 'pulse', [(i, i ^ mask) for i in range(count)])]
    another operation x1 -> x0, local copies, waits for them, and re-layouts: 1.06 us -> none  [body(): signal = signal.reshape(4, beams // 4, 2, bins).transpose(0, 2, 1, 3)]
    unnamed x0 -> x1, local copies, waits for them, and re-layouts: none -> 1.06 us
    ppermute x5 -> x4, waiting for transfers between devices: 0.57 us -> 0.66 us  [sent(): return lax.ppermute(array, 'pulse', [(i, i ^ mask) for i in range(count)])]
  transfers between devices with their start and end apart: 6 -> 5, of which waited for: 2 -> 1; matrix products, arithmetic and copies ran while one was open for 0% -> 0% of each run, Pallas kernels for 17% -> 20%
where the time goes in v4:
time: 25.1 us; the launch traced here: 24.9 us
  starting transfers between devices  11.1 us (44%)
  Pallas kernels  10.7 us (43%)
  local copies, waits for them, and re-layouts  2.26 us (9%)
  waiting for transfers between devices  0.66 us (3%)
    ppermute x4, starting transfers between devices, sent(): return lax.ppermute(array, 'pulse', [(i, i ^ mask) for i in range(count)])  8.11 us
    pallas_call x1, Pallas kernels, body(): pl.pallas_call(second_kernel(bins), out_shape=jax.ShapeDtypeStruct((2, 2...  5.78 us
    ppermute x1, starting transfers between devices, neighbours(): first = lax.ppermute(jnp.where(even, tail, head), axis, near)  3.03 us
    pallas_call x1, Pallas kernels, body(): pl.pallas_call(first_kernel(bins), out_shape=jax.ShapeDtypeStruct((ONE, T...  2.79 us
    pallas_call x1, Pallas kernels, body(): pl.pallas_call(prep_kernel(bins), out_shape=(jax.ShapeDtypeStruct((span,...  2.11 us
    broadcast_in_dim x1, local copies, waits for them, and re-layouts, body(): return image.transpose(1, 0, 2)[None, None]  1.15 us
    unnamed x1, local copies, waits for them, and re-layouts  1.06 us
    ppermute x4, waiting for transfers between devices, sent(): return lax.ppermute(array, 'pulse', [(i, i ^ mask) for i in range(count)])  0.66 us
  transfers between devices with their start and end apart: 5, of which 1 were waited for; matrix products, arithmetic and copies ran while one was open for 0% of the time, Pallas kernels for 20%

profile of v4, /device:TPU:0, one launch (start us, length us, event | category | flops | bytes accessed | tf_op | source)
XLA Modules:
  0.0 24.9 jit_solution(1520068547937425349)
XLA Ops:
  0.0 1.1 %copy.18 = bf16[1,32,2,3072]{3,1,2,0:T(8,128)(2,1)S(1)} copy(bf16[1,32,2,3072]{3,2,1,0:T(2,128)(2,1)} %param.10) | data formatting | bytes 786432 | tf_op args[0]
  1.1 3.0 %collective-permute-start = (bf16[4,2,8,640]{3,2,0,1:T(8,128)(2,1)S(1)}, bf16[4,2,8,640]{3,2,0,1:T(8,128)(2,1)S(1)}, u32[]{:S(2)}, u32[]{:S(2)}) collective-permute-start(bf16[4,2,8,640]{3,2,0,1:T(8,128)(2,1)S(1)} %slice_select_fusion), channel_id=1, source_target_pairs={{0,2},{2,0},{1,3},{3,1},{4,6},{6,4},{5,7},{7,5},{8,10},{10,8},{9,1... | collective-permute-start | bytes 245768 | tf_op jit(solution)/shard_map/ppermute | solution.py:328
  4.1 3.7 %collective-permute-start.2 = (bf16[2,8,3072]{2,1,0:T(8,128)(2,1)S(1)}, bf16[2,8,3072]{2,1,0:T(8,128)(2,1)S(1)}, u32[]{:S(2)}, u32[]{:S(2)}) collective-permute-start(bf16[2,8,3072]{2,1,0:T(8,128)(2,1)S(1)} %dynamic-slice_bitcast_fusion.3), channel_id=1, source_target_pairs={{0,12},{4,8},{8,4},{12,0},{1,13},{5,9},{9,5},{13,1},{2,14},{6,10},... | collective-permute-start | bytes 294920 | tf_op jit(solution)/shard_map/ppermute | solution.py:355
  7.8 0.0 collective-permute-done
  7.9 0.9 %collective-permute-start.4 = (bf16[2,8,3840]{2,1,0:T(8,128)(2,1)S(1)}, bf16[2,8,3840]{2,1,0:T(8,128)(2,1)S(1)}, u32[]{:S(2)}, u32[]{:S(2)}) collective-permute-start(bf16[2,8,3840]{2,1,0:T(8,128)(2,1)S(1)} %get-tuple-element.11), channel_id=1, source_target_pairs={{0,4},{4,0},{8,12},{12,8},{1,5},{5,1},{9,13},{13,9},{2,6},{6,2},{1... | collective-permute-start | bytes 368648 | tf_op jit(solution)/shard_map/ppermute | solution.py:355
  8.8 2.6 %collective-permute-start.1 = (bf16[2,8,3840]{2,1,0:T(8,128)(2,1)S(1)}, bf16[2,8,3840]{2,1,0:T(8,128)(2,1)S(1)}, u32[]{:S(2)}, u32[]{:S(2)}) collective-permute-start(bf16[2,8,3840]{2,1,0:T(8,128)(2,1)S(1)} %get-tuple-element.13), channel_id=1, source_target_pairs={{0,8},{4,12},{8,0},{12,4},{1,9},{5,13},{9,1},{13,5},{2,10},{6,14},... | collective-permute-start | bytes 368648 | tf_op jit(solution)/shard_map/ppermute | solution.py:355
  11.4 0.9 %collective-permute-start.3 = (bf16[2,8,768]{2,1,0:T(8,128)(2,1)S(1)}, bf16[2,8,768]{2,1,0:T(8,128)(2,1)S(1)}, u32[]{:S(2)}, u32[]{:S(2)}) collective-permute-start(bf16[2,8,768]{2,1,0:T(8,128)(2,1)S(1)} %fusion.1), channel_id=1, source_target_pairs={{0,12},{4,8},{8,4},{12,0},{1,13},{5,9},{9,5},{13,1},{2,14},{6,10},... | collective-permute-start | bytes 73736 | tf_op jit(solution)/shard_map/ppermute | solution.py:355
  12.4 2.1 %prepare.1 = (bf16[640,256]{1,0:T(8,128)(2,1)S(1)}, f32[96,8,128]{2,1,0:T(8,128)S(1)}, f32[96,2,56,128]{3,2,1,0:T(8,128)S(1)}) custom-call(bf16[2,512]{1,0:T(2,128)(2,1)} %refs_0_.1, s32[2,128]{1,0:T(2,128)} %far_shift_one.1, f32[2,128]{1,0:T(2,128)} %refs_2_.1, f32[2,128]{1,0:T(2,128)} %refs_3_.1, s32[2,256]{1,0:T(2,128)} %far_shift_two.1, ...), custom_call_target="tpu_custom_call" | custom-call | tf_op jit(solution)/shard_map/prepare/pallas_call | solution.py:377
  14.5 0.7 %collective-permute-done.4.a1 = bf16[2,8,3840]{2,1,0:T(8,128)(2,1)S(1)} collective-permute-done((bf16[2,8,3840]{2,1,0:T(8,128)(2,1)S(1)}, bf16[2,8,3840]{2,1,0:T(8,128)(2,1)S(1)}, u32[]{:S(2)}, u32[]{:S(2)}) %collective-permute-start.4) | collective-permute-done | bytes 122912 | tf_op jit(solution)/shard_map/ppermute | solution.py:355
  15.1 2.8 %first_pair.1.done_ref = f32[16,120,128]{2,1,0:T(8,128)S(1)} custom-call(s32[2,128]{1,0:T(2,128)} %far_beam_one.1, s32[2,128]{1,0:T(2,128)} %far_shift_one.1, bf16[2,8,3840]{2,1,0:T(8,128)(2,1)S(1)} %get-tuple-element.12.a0, bf16[2,8,3840]{2,1,0:T(8,128)(2,1)S(1)} %collective-permute-done.4.a1, bf16[640,256]{1,0:T(8,128)(2,1)S(1)} %get-tuple-element.8.band_ref, ...), custom_call_target="tpu_custom_call" | custom-call | tf_op jit(solution)/shard_map/first_pair/pallas_call | solution.py:398
  17.9 0.0 collective-permute-done.2.a3
  18.0 0.0 collective-permute-done.3.r3
  18.0 0.0 collective-permute-done.1.a2
  18.0 5.8 %second_pair.1 = bf16[2,32,3072]{2,1,0:T(8,128)(2,1)S(1)} custom-call(s32[2,128]{1,0:T(2,128)} %far_beam_one.1, s32[2,128]{1,0:T(2,128)} %far_shift_one.1, s32[2,256]{1,0:T(2,128)} %far_beam_two.1, s32[2,256]{1,0:T(2,128)} %far_shift_two.1, bf16[2,8,3840]{2,1,0:T(8,128)(2,1)S(1)} %collective-permute-done.1.a2, ...), custom_call_target="tpu_custom_call" | custom-call | tf_op jit(solution)/shard_map/second_pair/pallas_call | solution.py:407
  23.8 1.2 %copy.14 = bf16[1,1,32,2,3072]{4,3,2,1,0:T(2,128)(2,1)} copy(bf16[1,1,32,2,3072]{4,2,3,1,0:T(8,128)(2,1)S(1)} %bitcast.23) | data formatting | bytes 786432 | tf_op jit(solution)/shard_map/broadcast_in_dim | solution.py:424
  (7 shorter events, 0.1 us)
Async XLA Ops:
  1.1 6.7 %collective-permute-start = (bf16[4,2,8,640]{3,2,0,1:T(8,128)(2,1)S(1)}, bf16[4,2,8,640]{3,2,0,1:T(8,128)(2,1)S(1)}, u32[]{:S(2)}, u32[]{:S(2)}) collective-permute-start(bf16[4,2,8,640]{3,2,0,1:T(8,128)(2,1)S(1)} %slice_select_fusion), channel_id=1, source_target_pairs={{0,2},{2,0},{1,3},{3,1},{4,6},{6,4},{5,7},{7,5},{8,10},{10,8},{9,1... | collective-permute-start | bytes 245768 | tf_op jit(solution)/shard_map/ppermute | solution.py:328
  4.1 13.8 %collective-permute-start.2 = (bf16[2,8,3072]{2,1,0:T(8,128)(2,1)S(1)}, bf16[2,8,3072]{2,1,0:T(8,128)(2,1)S(1)}, u32[]{:S(2)}, u32[]{:S(2)}) collective-permute-start(bf16[2,8,3072]{2,1,0:T(8,128)(2,1)S(1)} %dynamic-slice_bitcast_fusion.3), channel_id=1, source_target_pairs={{0,12},{4,8},{8,4},{12,0},{1,13},{5,9},{9,5},{13,1},{2,14},{6,10},... | collective-permute-start | bytes 294920 | tf_op jit(solution)/shard_map/ppermute | solution.py:355
  7.9 7.2 %collective-permute-start.4 = (bf16[2,8,3840]{2,1,0:T(8,128)(2,1)S(1)}, bf16[2,8,3840]{2,1,0:T(8,128)(2,1)S(1)}, u32[]{:S(2)}, u32[]{:S(2)}) collective-permute-start(bf16[2,8,3840]{2,1,0:T(8,128)(2,1)S(1)} %get-tuple-element.11), channel_id=1, source_target_pairs={{0,4},{4,0},{8,12},{12,8},{1,5},{5,1},{9,13},{13,9},{2,6},{6,2},{1... | collective-permute-start | bytes 368648 | tf_op jit(solution)/shard_map/ppermute | solution.py:355
  8.8 9.1 %collective-permute-start.1 = (bf16[2,8,3840]{2,1,0:T(8,128)(2,1)S(1)}, bf16[2,8,3840]{2,1,0:T(8,128)(2,1)S(1)}, u32[]{:S(2)}, u32[]{:S(2)}) collective-permute-start(bf16[2,8,3840]{2,1,0:T(8,128)(2,1)S(1)} %get-tuple-element.13), channel_id=1, source_target_pairs={{0,8},{4,12},{8,0},{12,4},{1,9},{5,13},{9,1},{13,5},{2,10},{6,14},... | collective-permute-start | bytes 368648 | tf_op jit(solution)/shard_map/ppermute | solution.py:355
  11.4 6.5 %collective-permute-start.3 = (bf16[2,8,768]{2,1,0:T(8,128)(2,1)S(1)}, bf16[2,8,768]{2,1,0:T(8,128)(2,1)S(1)}, u32[]{:S(2)}, u32[]{:S(2)}) collective-permute-start(bf16[2,8,768]{2,1,0:T(8,128)(2,1)S(1)} %fusion.1), channel_id=1, source_target_pairs={{0,12},{4,8},{8,4},{12,0},{1,13},{5,9},{9,5},{13,1},{2,14},{6,10},... | collective-permute-start | bytes 73736 | tf_op jit(solution)/shard_map/ppermute | solution.py:355
